TPU v7x, 128 devices: a whole 4x4x4 slice. The times are simulated.
128 devices in a mesh: tm: 4 (over x), row: 32 (over z, y, core).
Axes of the slice: x: 4, y: 4, z: 4, core: 2. Of those that a mesh axis runs over, the one named last changes fastest.
Arguments:
- coupling: float32 [4, 8192, 8192], P('tm', 'row'), may hold values from -0.0625 to 0.0625
- damping: float32 [4, 8192], P('tm', 'row'), may hold values from 0.5 to 3
- forcing: float32 [4, 8, 8192], P('tm', None, 'row'), may hold values from -6 to 6
- initial: float32 [8, 8192], P(None, 'row'), may hold values from -6 to 6
- counts: int32 [4], P('tm'), may hold values from 1 to 8
Outputs:
- states: float32 [4, 8, 8192], P('tm', None, 'row')
All inputs are finite; a program needn't handle non-finite values.
Results may differ from a plain program's by a relative error of at most 0.00013.
Values sent between devices are 32-bit elements; how exact they have to be, the bound alone decides.
A program may use at most 64 MiB of HBM per device.

v0:
```python
import jax
import jax.numpy as jnp
from jax import lax
from jax.sharding import PartitionSpec as P

KRYLOV = 2


time_step = 0.125
epsilon = 1e-06
squarings = 5
taylor_terms = 12
highest = lax.Precision.HIGHEST


def from_everyone(array, axis):
    size = lax.axis_size(axis)
    return lax.all_to_all(
        jnp.broadcast_to(array[None], (size, *array.shape)), axis, 0, 0, tiled=True
    )


def in_order(pieces, dim):
    pieces = jnp.moveaxis(pieces, 0, dim)
    lengths = pieces.shape
    return pieces.reshape(*lengths[:dim], lengths[dim] * lengths[dim + 1], *lengths[dim + 2 :])


def collect(array, axis, dim):
    pieces = from_everyone(array, axis)
    return in_order(pieces, dim)


def side_by_side(arrays, axis, dim, along):
    ends, at = ([], 0)
    for a in arrays[:-1]:
        at += a.shape[along]
        ends.append(at)
    both = jnp.concatenate(arrays, axis=along)
    return tuple(jnp.split(lax.all_gather(both, axis, axis=dim, tiled=True), ends, axis=along))


def passed_along(array, axis, by):
    size = lax.axis_size(axis)
    pairs = [(i, i + by) for i in range(size) if 0 <= i + by < size]
    return lax.ppermute(array, axis, pairs)


def matrix_exponential(matrix):
    scaled = matrix / 2.0**squarings
    dimension = matrix.shape[-1]
    identity = jnp.broadcast_to(jnp.eye(dimension, dtype=jnp.float32), matrix.shape)
    result = identity
    for degree in range(taylor_terms, 0, -1):
        result = identity + jnp.einsum("bij,bjk->bik", scaled, result, precision=highest) / degree
    for repeat in range(squarings):
        result = jnp.einsum("bij,bjk->bik", result, result, precision=highest)
    return result


def exponent_block(hessenberg, step_size):
    members = hessenberg.shape[0]
    augmented = jnp.zeros((members, KRYLOV + 1, KRYLOV + 1), jnp.float32)
    augmented = augmented.at[:, :KRYLOV, :KRYLOV].set(step_size * hessenberg)
    augmented = augmented.at[:, 0, KRYLOV].set(1.0)
    return matrix_exponential(augmented)


def rows_product(vectors, local_coupling):
    return lax.dot_general(
        vectors,
        local_coupling,
        (((1,), (1,)), ((), ())),
        precision=highest,
        preferred_element_type=jnp.float32,
    )


def combine_basis(krylov_basis, coefficients):
    return jnp.einsum("kbn,bk->bn", krylov_basis, coefficients, precision=highest)


def whole_arnoldi(vectors, local_coupling, local_damping, row_offset):
    members = vectors.shape[0]
    extent = vectors.shape[1]
    rows_local = local_coupling.shape[0]
    start_norm = jnp.sqrt(jnp.sum(vectors * vectors, axis=1) + epsilon)
    krylov_basis = (
        jnp.zeros((KRYLOV, members, extent), jnp.float32).at[0].set(vectors / start_norm[:, None])
    )
    hessenberg = jnp.zeros((members, KRYLOV, KRYLOV), jnp.float32)
    for column in range(KRYLOV):
        current = krylov_basis[column]
        own_rows = lax.dynamic_slice_in_dim(current, row_offset, rows_local, 1)
        applied_rows = rows_product(current, local_coupling) - local_damping * own_rows
        applied = collect(applied_rows, "row", 1)
        weights = jnp.einsum("kbn,bn->kb", krylov_basis, applied, precision=highest)
        applied = applied - jnp.einsum("kb,kbn->bn", weights, krylov_basis, precision=highest)
        hessenberg = hessenberg.at[:, :, column].set(weights.T)
        if column + 1 < KRYLOV:
            length = jnp.sqrt(jnp.sum(applied * applied, axis=1) + epsilon)
            krylov_basis = krylov_basis.at[column + 1].set(applied / length[:, None])
            hessenberg = hessenberg.at[:, column + 1, column].set(length)
    return (start_norm, krylov_basis, hessenberg)


def on_device(coupling, damping, forcing, initial, counts):
    local_coupling = coupling[0]
    local_damping = damping[0]
    local_forcing = forcing[0]
    rows_local = local_coupling.shape[0]
    members = initial.shape[0]
    step_size = counts[0].astype(jnp.float32) * time_step
    slab_index = lax.axis_index("tm")
    row_offset = lax.axis_index("row") * rows_local
    sections = lax.axis_size("tm")

    def run_arnoldi(vectors):
        outcome = whole_arnoldi(vectors, local_coupling, local_damping, row_offset)
        return outcome

    def carried_term(norms, krylov_basis, hessenberg):
        block = exponent_block(hessenberg, step_size)
        return combine_basis(krylov_basis, norms[:, None] * block[:, :KRYLOV, 0])

    forcing_vectors, incoming = side_by_side((local_forcing, initial), "row", 1, 0)
    norms, krylov_basis, hessenberg = run_arnoldi(
        jnp.concatenate([forcing_vectors, incoming], axis=0)
    )
    local_norms = norms[:members]
    local_krylov_basis = krylov_basis[:, :members]
    local_hessenberg = hessenberg[:members]
    block = exponent_block(local_hessenberg, step_size)
    local_part = combine_basis(
        local_krylov_basis, (step_size * local_norms)[:, None] * block[:, :KRYLOV, KRYLOV]
    )
    section_zero = (
        carried_term(norms[members:], krylov_basis[:, members:], hessenberg[members:]) + local_part
    )
    result = jnp.zeros_like(incoming)
    for section in range(sections):
        if section == 0:
            outgoing = section_zero
        else:
            carried_norm, carried_basis, carried_hessenberg = run_arnoldi(incoming)
            outgoing = carried_term(carried_norm, carried_basis, carried_hessenberg) + local_part
        result = jnp.where(slab_index == section, outgoing, result)
        if section + 1 < sections:
            incoming = passed_along(outgoing, "tm", 1)
    result = lax.dynamic_slice_in_dim(result, row_offset, rows_local, 1)
    return result[None]


def solution(mesh):
    placed = (P("tm", "row", None), P("tm", "row"), P("tm", None, "row"), P(None, "row"), P("tm"))
    return jax.shard_map(
        on_device, mesh=mesh, in_specs=placed, out_specs=P("tm", None, "row"), check_vma=False
    )
```

profile of v0, /device:TPU:6, one launch (start us, length us, event | category | flops | bytes accessed | tf_op | source)
XLA Modules:
  0.0 354.9 jit_solution(14266680646369196260)
XLA Ops:
  0.7 26.3 %all_gather.3 = f32[16,8192]{1,0:T(8,128)S(1)} all-gather(f32[16,256]{1,0:T(8,128)S(1)} %pad_maximum_fusion.4), channel_id=1, replica_groups=mesh['tm'=4,'row'=32] {'row'}, dimensions={1}, use_global_device_ids=true | all-gather | bytes 540672 | tf_op jit(solution)/shard_map/all_gather | solution.py:40
  27.3 8.9 %fusion.16 = f32[16,256]{1,0:T(8,128)S(1)} fusion(f32[16,8192]{1,0:T(8,128)S(1)} %broadcast_divide_fusion.1, f32[1,256,8192]{2,1,0:T(8,128)} %param.65, s32[]{:T(128)S(6)} %select_n.38, f32[256]{0:T(256)} %bitcast.408), kind=kOutput, calls=%fused_computation.21 | convolution fusion | flops 402661376 | bytes 8946692 | tf_op jit(solution)/shard_map/dot_general | solution.py:70
  37.2 5.4 %all-to-all-start = ((f32[32,16,256]{2,1,0:T(8,128)}), f32[32,16,256]{2,1,0:T(8,128)S(1)}, u32[]{:S(2)}, u32[]{:S(2)}) async-start(f32[32,16,256]{2,1,0:T(8,128)} %broadcast_in_dim.202), calls=%async_computation | async-start | bytes 1048576 | tf_op jit(solution)/shard_map/all_to_all | solution.py:18
  45.3 9.0 %all-to-all-done = f32[32,16,256]{2,1,0:T(8,128)S(1)} async-done(((f32[32,16,256]{2,1,0:T(8,128)}), f32[32,16,256]{2,1,0:T(8,128)S(1)}, u32[]{:S(2)}, u32[]{:S(2)}) %all-to-all-start) | async-done | bytes 524320 | tf_op jit(solution)/shard_map/all_to_all | solution.py:18
  55.2 8.8 %fusion.97 = f32[16,1,2]{2,1,0:T(1,128)S(1)} fusion(f32[16,8192,1]{1,2,0:T(1,128)S(1)} %reshape.1045, f32[1,16,8192]{2,0,1:T(1,128)S(1)} %copy.159), kind=kOutput, calls=%fused_computation.146 | convolution fusion | flops 3145728 | bytes 1048704 | tf_op jit(solution)/shard_map/kbn,bn->kb/dot_general | solution.py:97
  64.1 3.7 %fusion.95 = f32[16,1,8192]{2,1,0:T(1,128)S(1)} fusion(f32[2,16,1]{0,2,1:T(1,128)S(1)} %copy.113, f32[1,16,8192]{2,0,1:T(1,128)S(1)} %copy.159), kind=kOutput, calls=%fused_computation.144 | convolution fusion | flops 3145728 | bytes 1048704 | tf_op jit(solution)/shard_map/kb,kbn->bn/dot_general | solution.py:98
  68.7 9.3 %fusion.19 = f32[16,256]{1,0:T(8,128)S(1)} fusion(f32[16,8192]{1,0:T(8,128)S(1)} %broadcast_divide_fusion, f32[1,256,8192]{2,1,0:T(8,128)} %param.65, s32[]{:T(128)S(6)} %select_n.38, f32[256]{0:T(256)S(1)} %bitcast.409), kind=kOutput, calls=%fused_computation.22 | convolution fusion | flops 402661376 | bytes 8946692 | tf_op jit(solution)/shard_map/dot_general | solution.py:70
  78.9 3.9 %all-to-all-start.1 = ((f32[32,16,256]{2,1,0:T(8,128)}), f32[32,16,256]{2,1,0:T(8,128)S(1)}, u32[]{:S(2)}, u32[]{:S(2)}) async-start(f32[32,16,256]{2,1,0:T(8,128)} %broadcast_in_dim.204), calls=%async_computation.1 | async-start | bytes 1048576 | tf_op jit(solution)/shard_map/all_to_all | solution.py:18
  83.8 10.8 %all-to-all-done.1 = f32[32,16,256]{2,1,0:T(8,128)S(1)} async-done(((f32[32,16,256]{2,1,0:T(8,128)}), f32[32,16,256]{2,1,0:T(8,128)S(1)}, u32[]{:S(2)}, u32[]{:S(2)}) %all-to-all-start.1) | async-done | bytes 524320 | tf_op jit(solution)/shard_map/all_to_all | solution.py:18
  95.4 9.4 %fusion.99 = f32[16,1,2]{2,1,0:T(1,128)S(1)} fusion(f32[16,8192,1]{1,2,0:T(1,128)S(1)} %reshape.1047, f32[2,16,8192]{2,1,0:T(8,128)S(1)} %pad_maximum_fusion), kind=kOutput, calls=%fused_computation.148 | convolution fusion | flops 3145728 | bytes 1572992 | tf_op jit(solution)/shard_map/kbn,bn->kb/dot_general | solution.py:97
  117.1 3.1 fusion.115
  120.2 2.1 fusion.117
  123.8 8.9 %collective-permute-done = f32[8,8192]{1,0:T(8,128)S(1)} collective-permute-done((f32[8,8192]{1,0:T(8,128)S(1)}, f32[8,8192]{1,0:T(8,128)S(1)}, u32[]{:S(2)}, u32[]{:S(2)}) %collective-permute-start) | collective-permute-done | bytes 262176 | tf_op jit(solution)/shard_map/ppermute | solution.py:46
  133.0 8.9 %fusion.77 = f32[8,256]{1,0:T(8,128)S(1)} fusion(f32[8,8192]{1,0:T(8,128)S(1)} %broadcast_divide_fusion.7, f32[1,256,8192]{2,1,0:T(8,128)} %param.65, s32[]{:T(128)S(6)} %select_n.38, f32[256]{0:T(256)S(1)} %bitcast.410), kind=kOutput, calls=%fused_computation.138 | convolution fusion | flops 201330688 | bytes 8668164 | tf_op jit(solution)/shard_map/dot_general | solution.py:70
  142.7 4.1 %all-to-all-start.2 = ((f32[32,8,256]{2,1,0:T(8,128)}), f32[32,8,256]{2,1,0:T(8,128)S(1)}, u32[]{:S(2)}, u32[]{:S(2)}) async-start(f32[32,8,256]{2,1,0:T(8,128)} %broadcast_in_dim.205), calls=%async_computation.2 | async-start | bytes 524288 | tf_op jit(solution)/shard_map/all_to_all | solution.py:18
  147.1 8.5 %all-to-all-done.2 = f32[32,8,256]{2,1,0:T(8,128)S(1)} async-done(((f32[32,8,256]{2,1,0:T(8,128)}), f32[32,8,256]{2,1,0:T(8,128)S(1)}, u32[]{:S(2)}, u32[]{:S(2)}) %all-to-all-start.2) | async-done | bytes 262176 | tf_op jit(solution)/shard_map/all_to_all | solution.py:18
  155.6 4.7 %fusion.111 = f32[8,1,2]{2,1,0:T(1,128)S(1)} fusion(f32[1,8,8192]{2,0,1:T(1,128)S(1)} %copy.160, f32[8,8192,1]{1,0,2:T(8,128)S(1)} %bitcast.390), kind=kOutput, calls=%fused_computation.160 | convolution fusion | flops 1572864 | bytes 524352 | tf_op jit(solution)/shard_map/kbn,bn->kb/dot_general | solution.py:97
  160.5 1.9 fusion.109
  162.9 8.9 %fusion.80 = f32[8,256]{1,0:T(8,128)S(1)} fusion(f32[8,8192]{1,0:T(8,128)S(1)} %broadcast_divide_fusion.6, f32[1,256,8192]{2,1,0:T(8,128)} %param.65, s32[]{:T(128)S(6)} %select_n.38, f32[256]{0:T(256)S(1)} %bitcast.411), kind=kOutput, calls=%fused_computation.139 | convolution fusion | flops 201330688 | bytes 8668164 | tf_op jit(solution)/shard_map/dot_general | solution.py:70
  172.5 3.9 %all-to-all-start.3 = ((f32[32,8,256]{2,1,0:T(8,128)}), f32[32,8,256]{2,1,0:T(8,128)S(1)}, u32[]{:S(2)}, u32[]{:S(2)}) async-start(f32[32,8,256]{2,1,0:T(8,128)} %broadcast_in_dim.206), calls=%async_computation.3 | async-start | bytes 524288 | tf_op jit(solution)/shard_map/all_to_all | solution.py:18
  176.9 8.4 %all-to-all-done.3 = f32[32,8,256]{2,1,0:T(8,128)S(1)} async-done(((f32[32,8,256]{2,1,0:T(8,128)}), f32[32,8,256]{2,1,0:T(8,128)S(1)}, u32[]{:S(2)}, u32[]{:S(2)}) %all-to-all-start.3) | async-done | bytes 262176 | tf_op jit(solution)/shard_map/all_to_all | solution.py:18
  185.3 4.9 %fusion.129 = f32[8,1,2]{2,1,0:T(1,128)S(1)} fusion(f32[2,8,8192]{2,1,0:T(8,128)S(1)} %pad_maximum_fusion.1, f32[8,8192,1]{1,0,2:T(8,128)S(1)} %bitcast.406), kind=kOutput, calls=%fused_computation.184 | convolution fusion | flops 1572864 | bytes 786496 | tf_op jit(solution)/shard_map/kbn,bn->kb/dot_general | solution.py:97
  190.3 1.9 broadcast_select_fusion.2
  197.2 2.1 fusion.127
  200.8 9.1 %collective-permute-done.1 = f32[8,8192]{1,0:T(8,128)S(1)} collective-permute-done((f32[8,8192]{1,0:T(8,128)S(1)}, f32[8,8192]{1,0:T(8,128)S(1)}, u32[]{:S(2)}, u32[]{:S(2)}) %collective-permute-start.1) | collective-permute-done | bytes 262176 | tf_op jit(solution)/shard_map/ppermute | solution.py:46
  210.2 8.9 %fusion.83 = f32[8,256]{1,0:T(8,128)S(1)} fusion(f32[8,8192]{1,0:T(8,128)S(1)} %broadcast_divide_fusion.5, f32[1,256,8192]{2,1,0:T(8,128)} %param.65, s32[]{:T(128)S(6)} %select_n.38, f32[256]{0:T(256)S(1)} %bitcast.412), kind=kOutput, calls=%fused_computation.140 | convolution fusion | flops 201330688 | bytes 8668164 | tf_op jit(solution)/shard_map/dot_general | solution.py:70
  219.9 4.0 %all-to-all-start.4 = ((f32[32,8,256]{2,1,0:T(8,128)}), f32[32,8,256]{2,1,0:T(8,128)S(1)}, u32[]{:S(2)}, u32[]{:S(2)}) async-start(f32[32,8,256]{2,1,0:T(8,128)} %broadcast_in_dim.207), calls=%async_computation.4 | async-start | bytes 524288 | tf_op jit(solution)/shard_map/all_to_all | solution.py:18
  224.3 8.5 %all-to-all-done.4 = f32[32,8,256]{2,1,0:T(8,128)S(1)} async-done(((f32[32,8,256]{2,1,0:T(8,128)}), f32[32,8,256]{2,1,0:T(8,128)S(1)}, u32[]{:S(2)}, u32[]{:S(2)}) %all-to-all-start.4) | async-done | bytes 262176 | tf_op jit(solution)/shard_map/all_to_all | solution.py:18
  232.8 4.7 %fusion.107 = f32[8,1,2]{2,1,0:T(1,128)S(1)} fusion(f32[1,8,8192]{2,0,1:T(1,128)S(1)} %copy.161, f32[8,8192,1]{1,0,2:T(8,128)S(1)} %bitcast.393), kind=kOutput, calls=%fused_computation.156 | convolution fusion | flops 1572864 | bytes 524352 | tf_op jit(solution)/shard_map/kbn,bn->kb/dot_general | solution.py:97
  237.7 1.9 fusion.105
  240.0 8.9 %fusion.86 = f32[8,256]{1,0:T(8,128)S(1)} fusion(f32[8,8192]{1,0:T(8,128)S(1)} %broadcast_divide_fusion.4, f32[1,256,8192]{2,1,0:T(8,128)} %param.65, s32[]{:T(128)S(6)} %select_n.38, f32[256]{0:T(256)S(1)} %bitcast.413), kind=kOutput, calls=%fused_computation.141 | convolution fusion | flops 201330688 | bytes 8668164 | tf_op jit(solution)/shard_map/dot_general | solution.py:70
  249.7 3.9 %all-to-all-start.5 = ((f32[32,8,256]{2,1,0:T(8,128)}), f32[32,8,256]{2,1,0:T(8,128)S(1)}, u32[]{:S(2)}, u32[]{:S(2)}) async-start(f32[32,8,256]{2,1,0:T(8,128)} %broadcast_in_dim.208), calls=%async_computation.5 | async-start | bytes 524288 | tf_op jit(solution)/shard_map/all_to_all | solution.py:18
  253.9 8.6 %all-to-all-done.5 = f32[32,8,256]{2,1,0:T(8,128)S(1)} async-done(((f32[32,8,256]{2,1,0:T(8,128)}), f32[32,8,256]{2,1,0:T(8,128)S(1)}, u32[]{:S(2)}, u32[]{:S(2)}) %all-to-all-start.5) | async-done | bytes 262176 | tf_op jit(solution)/shard_map/all_to_all | solution.py:18
  262.5 4.9 %fusion.125 = f32[8,1,2]{2,1,0:T(1,128)S(1)} fusion(f32[2,8,8192]{2,1,0:T(8,128)S(1)} %pad_maximum_fusion.2, f32[8,8192,1]{1,0,2:T(8,128)S(1)} %bitcast.407), kind=kOutput, calls=%fused_computation.180 | convolution fusion | flops 1572864 | bytes 786496 | tf_op jit(solution)/shard_map/kbn,bn->kb/dot_general | solution.py:97
  267.5 1.9 broadcast_select_fusion.1
  274.3 2.1 fusion.123
  278.2 8.9 %collective-permute-done.2 = f32[8,8192]{1,0:T(8,128)S(1)} collective-permute-done((f32[8,8192]{1,0:T(8,128)S(1)}, f32[8,8192]{1,0:T(8,128)S(1)}, u32[]{:S(2)}, u32[]{:S(2)}) %collective-permute-start.2) | collective-permute-done | bytes 262176 | tf_op jit(solution)/shard_map/ppermute | solution.py:46
  287.4 8.9 %fusion.89 = f32[8,256]{1,0:T(8,128)S(1)} fusion(f32[8,8192]{1,0:T(8,128)S(1)} %broadcast_divide_fusion.3, f32[1,256,8192]{2,1,0:T(8,128)} %param.65, s32[]{:T(128)S(6)} %select_n.38, f32[256]{0:T(256)S(1)} %bitcast.414), kind=kOutput, calls=%fused_computation.142 | convolution fusion | flops 201330688 | bytes 8668164 | tf_op jit(solution)/shard_map/dot_general | solution.py:70
  297.0 4.1 %all-to-all-start.6 = ((f32[32,8,256]{2,1,0:T(8,128)}), f32[32,8,256]{2,1,0:T(8,128)S(1)}, u32[]{:S(2)}, u32[]{:S(2)}) async-start(f32[32,8,256]{2,1,0:T(8,128)} %broadcast_in_dim.209), calls=%async_computation.6 | async-start | bytes 524288 | tf_op jit(solution)/shard_map/all_to_all | solution.py:18
  301.5 8.5 %all-to-all-done.6 = f32[32,8,256]{2,1,0:T(8,128)S(1)} async-done(((f32[32,8,256]{2,1,0:T(8,128)}), f32[32,8,256]{2,1,0:T(8,128)S(1)}, u32[]{:S(2)}, u32[]{:S(2)}) %all-to-all-start.6) | async-done | bytes 262176 | tf_op jit(solution)/shard_map/all_to_all | solution.py:18
  310.0 4.7 %fusion.103 = f32[8,1,2]{2,1,0:T(1,128)S(1)} fusion(f32[1,8,8192]{2,0,1:T(1,128)S(1)} %copy.162, f32[8,8192,1]{1,0,2:T(8,128)S(1)} %bitcast.396), kind=kOutput, calls=%fused_computation.152 | convolution fusion | flops 1572864 | bytes 524352 | tf_op jit(solution)/shard_map/kbn,bn->kb/dot_general | solution.py:97
  314.9 1.9 fusion.101
  317.3 8.9 %fusion.92 = f32[8,256]{1,0:T(8,128)S(1)} fusion(f32[8,8192]{1,0:T(8,128)S(1)} %broadcast_divide_fusion.2, f32[1,256,8192]{2,1,0:T(8,128)} %param.65, s32[]{:T(128)S(6)} %select_n.38, f32[256]{0:T(256)S(1)} %bitcast.415), kind=kOutput, calls=%fused_computation.143 | convolution fusion | flops 201330688 | bytes 8668164 | tf_op jit(solution)/shard_map/dot_general | solution.py:70
  326.9 3.9 %all-to-all-start.7 = ((f32[32,8,256]{2,1,0:T(8,128)}), f32[32,8,256]{2,1,0:T(8,128)S(1)}, u32[]{:S(2)}, u32[]{:S(2)}) async-start(f32[32,8,256]{2,1,0:T(8,128)} %broadcast_in_dim.210), calls=%async_computation.7 | async-start | bytes 524288 | tf_op jit(solution)/shard_map/all_to_all | solution.py:18
  331.2 8.5 %all-to-all-done.7 = f32[32,8,256]{2,1,0:T(8,128)S(1)} async-done(((f32[32,8,256]{2,1,0:T(8,128)}), f32[32,8,256]{2,1,0:T(8,128)S(1)}, u32[]{:S(2)}, u32[]{:S(2)}) %all-to-all-start.7) | async-done | bytes 262176 | tf_op jit(solution)/shard_map/all_to_all | solution.py:18
  339.7 4.9 %fusion.121 = f32[8,1,2]{2,1,0:T(1,128)S(1)} fusion(f32[2,8,8192]{2,1,0:T(8,128)S(1)} %pad_maximum_fusion.3, f32[8,8192,1]{1,0,2:T(8,128)S(1)} %bitcast.405), kind=kOutput, calls=%fused_computation.176 | convolution fusion | flops 1572864 | bytes 786496 | tf_op jit(solution)/shard_map/kbn,bn->kb/dot_general | solution.py:97
  344.7 1.9 broadcast_select_fusion
  351.6 2.1 fusion.119
  (218 shorter events, 50.2 us)
Async XLA Ops:
  0.0 44.5 %copy-start.1 = (s32[3]{0:T(128)S(1)}, s32[3]{0:T(128)}, u32[]{:S(2)}) copy-start(s32[3]{0:T(128)} %constant.763.clone.1) | copy-start | bytes 40
  36.3 32.4 %copy-start = (f32[1,256]{1,0:T(1,128)S(1)}, f32[1,256]{1,0:T(1,128)}, u32[]{:S(2)}) copy-start(f32[1,256]{1,0:T(1,128)} %param.66) | copy-start | bytes 3076
  37.2 17.2 %all-to-all-start = ((f32[32,16,256]{2,1,0:T(8,128)}), f32[32,16,256]{2,1,0:T(8,128)S(1)}, u32[]{:S(2)}, u32[]{:S(2)}) async-start(f32[32,16,256]{2,1,0:T(8,128)} %broadcast_in_dim.202), calls=%async_computation | async-start | bytes 1048576 | tf_op jit(solution)/shard_map/all_to_all | solution.py:18
  78.9 15.7 %all-to-all-start.1 = ((f32[32,16,256]{2,1,0:T(8,128)}), f32[32,16,256]{2,1,0:T(8,128)S(1)}, u32[]{:S(2)}, u32[]{:S(2)}) async-start(f32[32,16,256]{2,1,0:T(8,128)} %broadcast_in_dim.204), calls=%async_computation.1 | async-start | bytes 1048576 | tf_op jit(solution)/shard_map/all_to_all | solution.py:18
  122.5 10.2 %collective-permute-start = (f32[8,8192]{1,0:T(8,128)S(1)}, f32[8,8192]{1,0:T(8,128)S(1)}, u32[]{:S(2)}, u32[]{:S(2)}) collective-permute-start(f32[8,8192]{1,0:T(8,128)S(1)} %bitcast_add_fusion.2), channel_id=1, source_target_pairs={{0,32},{32,64},{64,96},{1,33},{33,65},{65,97},{2,34},{34,66},{66,9... | collective-permute-start | bytes 786440 | tf_op jit(solution)/shard_map/ppermute | solution.py:46
  142.7 13.0 %all-to-all-start.2 = ((f32[32,8,256]{2,1,0:T(8,128)}), f32[32,8,256]{2,1,0:T(8,128)S(1)}, u32[]{:S(2)}, u32[]{:S(2)}) async-start(f32[32,8,256]{2,1,0:T(8,128)} %broadcast_in_dim.205), calls=%async_computation.2 | async-start | bytes 524288 | tf_op jit(solution)/shard_map/all_to_all | solution.py:18
  172.5 12.8 %all-to-all-start.3 = ((f32[32,8,256]{2,1,0:T(8,128)}), f32[32,8,256]{2,1,0:T(8,128)S(1)}, u32[]{:S(2)}, u32[]{:S(2)}) async-start(f32[32,8,256]{2,1,0:T(8,128)} %broadcast_in_dim.206), calls=%async_computation.3 | async-start | bytes 524288 | tf_op jit(solution)/shard_map/all_to_all | solution.py:18
  199.5 10.4 %collective-permute-start.1 = (f32[8,8192]{1,0:T(8,128)S(1)}, f32[8,8192]{1,0:T(8,128)S(1)}, u32[]{:S(2)}, u32[]{:S(2)}) collective-permute-start(f32[8,8192]{1,0:T(8,128)S(1)} %bitcast_add_fusion.1), channel_id=1, source_target_pairs={{0,32},{32,64},{64,96},{1,33},{33,65},{65,97},{2,34},{34,66},{66,9... | collective-permute-start | bytes 786440 | tf_op jit(solution)/shard_map/ppermute | solution.py:46
  219.9 12.9 %all-to-all-start.4 = ((f32[32,8,256]{2,1,0:T(8,128)}), f32[32,8,256]{2,1,0:T(8,128)S(1)}, u32[]{:S(2)}, u32[]{:S(2)}) async-start(f32[32,8,256]{2,1,0:T(8,128)} %broadcast_in_dim.207), calls=%async_computation.4 | async-start | bytes 524288 | tf_op jit(solution)/shard_map/all_to_all | solution.py:18
  249.7 12.8 %all-to-all-start.5 = ((f32[32,8,256]{2,1,0:T(8,128)}), f32[32,8,256]{2,1,0:T(8,128)S(1)}, u32[]{:S(2)}, u32[]{:S(2)}) async-start(f32[32,8,256]{2,1,0:T(8,128)} %broadcast_in_dim.208), calls=%async_computation.5 | async-start | bytes 524288 | tf_op jit(solution)/shard_map/all_to_all | solution.py:18
  276.7 10.4 %collective-permute-start.2 = (f32[8,8192]{1,0:T(8,128)S(1)}, f32[8,8192]{1,0:T(8,128)S(1)}, u32[]{:S(2)}, u32[]{:S(2)}) collective-permute-start(f32[8,8192]{1,0:T(8,128)S(1)} %bitcast_add_fusion), channel_id=1, source_target_pairs={{0,32},{32,64},{64,96},{1,33},{33,65},{65,97},{2,34},{34,66},{66,9... | collective-permute-start | bytes 786440 | tf_op jit(solution)/shard_map/ppermute | solution.py:46
  297.0 13.0 %all-to-all-start.6 = ((f32[32,8,256]{2,1,0:T(8,128)}), f32[32,8,256]{2,1,0:T(8,128)S(1)}, u32[]{:S(2)}, u32[]{:S(2)}) async-start(f32[32,8,256]{2,1,0:T(8,128)} %broadcast_in_dim.209), calls=%async_computation.6 | async-start | bytes 524288 | tf_op jit(solution)/shard_map/all_to_all | solution.py:18
  326.9 12.8 %all-to-all-start.7 = ((f32[32,8,256]{2,1,0:T(8,128)}), f32[32,8,256]{2,1,0:T(8,128)S(1)}, u32[]{:S(2)}, u32[]{:S(2)}) async-start(f32[32,8,256]{2,1,0:T(8,128)} %broadcast_in_dim.210), calls=%async_computation.7 | async-start | bytes 524288 | tf_op jit(solution)/shard_map/all_to_all | solution.py:18
where the time goes:
time: 361 us; the launch traced here: 355 us
  matrix products  156 us (43%)
  waiting for transfers between devices  97.7 us (27%)
  starting transfers between devices  37 us (10%)
  blocking collectives  26.3 us (7%)
  local copies, waits for them, and re-layouts  20.1 us (6%)
  other arithmetic  15.4 us (4%)
    dot_general x8, matrix products, rows_product(): lax.dot_general(vectors, local_coupling, (((1,), (1,)), ((), ())), precis...  71.8 us
    all_to_all x8, waiting for transfers between devices, from_everyone(): lax.all_to_all(jnp.broadcast_to(array[None], (size, *array.shape)), axis,...  70.9 us
    dot_general x8, matrix products, whole_arnoldi(): weights = jnp.einsum('kbn,bn->kb', krylov_basis, applied, precision=highest)  47 us
    all_to_all x8, starting transfers between devices, from_everyone(): lax.all_to_all(jnp.broadcast_to(array[None], (size, *array.shape)), axis,...  33.1 us
    ppermute x3, waiting for transfers between devices, passed_along(): return lax.ppermute(array, axis, pairs)  26.9 us
    all_gather x1, blocking collectives, side_by_side(): lax.all_gather(both, axis, axis=dim, tiled=True)  26.3 us
    dot_general x60, matrix products, matrix_exponential(): jnp.einsum('bij,bjk->bik', scaled, result, precision=highest) / degree  11.3 us
    dot_general x5, matrix products, combine_basis(): jnp.einsum('kbn,bk->bn', krylov_basis, coefficients, precision=highest)  11.3 us
  transfers between devices with their start and end apart: 11, of which 11 were waited for; matrix products, arithmetic and copies ran while one was open for 2% of the time, Pallas kernels for 0%

commit v1 on v0

v1 whole, which is shorter than its diff:
```python
import functools

import jax
import jax.numpy as jnp
from jax import lax
from jax.experimental import pallas as pl
from jax.experimental.pallas import tpu as pltpu
from jax.sharding import PartitionSpec as P

MESH = pl.DeviceIdType.MESH
TIME_STEP = 0.125
EPSILON = 1e-06
SQUARINGS = 5
TAYLOR_TERMS = 12
SIDE = 4
LANES = 128
CHUNKS = 8


def offset(i):
    return lax.rem(2 + i + i // 2 + 2 * (i // 3), SIDE)


def exponential(h, g, below, above, corner):
    scale = h * (1.0 / 2.0**SQUARINGS)
    s00, s01, s10, s11 = g * scale, above * scale, below * scale, corner * scale
    edge = 1.0 / 2.0**SQUARINGS
    one, zero = jnp.ones_like(s00), jnp.zeros_like(s00)
    r00, r01, r10, r11, c0, c1 = one, zero, zero, one, zero, zero
    for degree in range(TAYLOR_TERMS, 0, -1):
        f = 1.0 / degree
        r00, r01, r10, r11, c0, c1 = (
            1.0 + (s00 * r00 + s01 * r10) * f,
            (s00 * r01 + s01 * r11) * f,
            (s10 * r00 + s11 * r10) * f,
            1.0 + (s10 * r01 + s11 * r11) * f,
            (s00 * c0 + s01 * c1 + edge) * f,
            (s10 * c0 + s11 * c1) * f,
        )
    for _ in range(SQUARINGS):
        r00, r01, r10, r11, c0, c1 = (
            r00 * r00 + r01 * r10,
            r00 * r01 + r01 * r11,
            r10 * r00 + r11 * r10,
            r10 * r01 + r11 * r11,
            r00 * c0 + r01 * c1 + c0,
            r10 * c0 + r11 * c1 + c1,
        )
    return r00, r10, c0, c1


def kernel(
    members, rows, parts, slabs,
    a_hbm, damp_ref, f_ref, c_ref, n_ref, o_ref,
    stage, at, xs, g0, gf, gu, lb, pr, ck, tb, tf, tp, ls, prs,
    a_sem, send, recv,
):
    t, r = lax.axis_index("tm"), lax.axis_index("row")
    core, chip = lax.rem(r, 2), r // 2
    z, y = chip // SIDE, lax.rem(chip, SIDE)
    width = a_hbm.shape[2] // CHUNKS
    G0, GF, GU, LBR, LB, PRR, PR, TF, TB, TP = range(10)

    def loads(j):
        return pltpu.make_async_copy(
            a_hbm.at[0, :, pl.ds(j * width, width)], stage.at[j], a_sem.at[j]
        )

    def copy(src, dst, k, device):
        return pltpu.make_async_remote_copy(
            src_ref=src, dst_ref=dst, send_sem=send.at[k], recv_sem=recv.at[k],
            device_id=device, device_id_type=MESH,
        )

    def other(i):
        zz, yy = lax.rem(z + offset(i // SIDE), SIDE), lax.rem(y + offset(lax.rem(i, SIDE)), SIDE)
        return 2 * (zz * SIDE + yy)

    def spread(src, dst, k):
        @pl.loop(0, parts // 2 - 1)
        def _(i):
            at_chip = other(i)
            copy(src, dst, k, (t, at_chip + core)).start()
            copy(src, dst, k, (t, at_chip + 1 - core)).start()

        copy(src, dst, k, (t, chip * 2 + 1 - core)).start()

    def spread_next(src, dst, k):
        @pl.loop(0, parts // 2)
        def _(i):
            at_chip = other(i)
            copy(src, dst, k, (t + 1, at_chip + core)).start()
            copy(src, dst, k, (t + 1, at_chip + 1 - core)).start()

    def arrived(buffer, k, count=parts - 1):
        some = buffer.at[pl.ds(0, count)]
        pltpu.make_async_copy(some, some, recv.at[k]).wait()

    def left(buffer, k, count=parts - 1):
        some = buffer.at[pl.ds(0, count)]
        pltpu.make_async_copy(some, some, send.at[k]).wait()

    def fill(slot, at_part, v):
        high = v.astype(jnp.bfloat16).astype(jnp.float32)
        both = jnp.concatenate([high, v - high], axis=0).astype(jnp.bfloat16)
        xs[16 * slot : 16 * slot + 16, rows * at_part : rows * at_part + rows] = both

    def product(count):
        d = jnp.dot(xs[0 : 16 * count, :], at[...], preferred_element_type=jnp.float32)
        out = []
        for j in range(count):
            top, low = d[16 * j : 16 * j + 8], d[16 * j + 8 : 16 * j + 16]
            out.append(top[:, :rows] + (top[:, rows:] + low[:, :rows]))
        return out

    damp = damp_ref[...]

    def moments(first, second):
        n2 = jnp.zeros((members, rows), jnp.float32)
        d = jnp.zeros((members, rows), jnp.float32)
        for p in range(parts):
            c = first(p)
            n2 += c * c
            d += c * second(p)
        b2 = jnp.sum(n2, axis=1, keepdims=True) + EPSILON
        return b2, jnp.sum(d, axis=1, keepdims=True) / b2

    def remainder(first, second, g, keep):
        w2 = jnp.zeros((members, rows), jnp.float32)
        for p in range(parts):
            w = second(p) - g * first(p)
            if keep:
                fill(0, p, w)
            w2 += w * w
        return jnp.sum(w2, axis=1, keepdims=True)

    def second_step(first, second, own_first, own_second):
        b2, g = moments(first, second)
        below = jnp.sqrt(remainder(first, second, g, True) / b2 + EPSILON)
        w = own_second - g * own_first
        image = product(1)[0] - damp * w
        t0 = jnp.sum(own_first * image, axis=1, keepdims=True)
        t1 = jnp.sum(w * image, axis=1, keepdims=True)
        return (b2, g, below), (t0, t1)

    lane = lax.broadcasted_iota(jnp.int32, (members, LANES), 1)
    member = lax.broadcasted_iota(jnp.int32, (members, LANES), 0)

    def packed(columns):
        row = jnp.zeros((members, LANES), jnp.float32)
        for j, column in enumerate(columns):
            if column is not None:
                row = jnp.where(lane == member + members * j, column, row)
        return jnp.sum(row, axis=0, keepdims=True)

    def unpacked(buffer, count):
        total = jnp.sum(buffer[...], axis=0)
        total = jnp.broadcast_to(total, (members, LANES))
        return [
            jnp.sum(jnp.where(lane == member + members * j, total, 0.0), axis=1, keepdims=True)
            for j in range(count)
        ]

    def start_weights(h, known, t0, t1):
        b2, g, below = known
        e00, e10, _, _ = exponential(h, g, below, t0 / (b2 * below), t1 / (b2 * below * below))
        x2 = e10 / below
        return e00 - g * x2, x2

    def forcing_weights(h, known, t0, t1):
        b2, g, below = known
        _, _, c0, c1 = exponential(h, g, below, t0 / (b2 * below), t1 / (b2 * below * below))
        x4 = h * c1 / below
        return h * c0 - g * x4, x4

    for j in range(CHUNKS):
        loads(j).start()
    barrier = pltpu.get_barrier_semaphore()

    @pl.loop(1, parts)
    def _(k):
        pl.semaphore_signal(
            barrier, inc=1, device_id=(t, lax.rem(r + k, parts)), device_id_type=MESH
        )

    for by in (1, -1):

        @pl.when(t + 1 < slabs if by == 1 else t > 0)
        def _():
            @pl.loop(0, parts)
            def _(k):
                pl.semaphore_signal(
                    barrier, inc=1, device_id=(t + by, lax.rem(r + k, parts)), device_id_type=MESH
                )

    h = jnp.full((members, 1), n_ref[0].astype(jnp.float32) * TIME_STEP, jnp.float32)
    g0[r] = jnp.concatenate([f_ref[...], c_ref[...]], axis=0)
    pl.semaphore_wait(barrier, parts - 1 + parts * (jnp.minimum(t, 1) + jnp.minimum(slabs - 1 - t, 1)))

    spread(g0.at[r], g0.at[r], G0)

    @pl.when(t == 0)
    def _():
        ls[...] = f_ref[...]
        copy(ls, lb.at[r], LBR, (t + 1, r)).start()

    for j in range(CHUNKS):
        loads(j).wait()
        for q in range(width // rows):
            block = stage[j, :, q * rows : (q + 1) * rows].T
            high = block.astype(jnp.bfloat16)
            at_row = j * width + q * rows
            at[at_row : at_row + rows, 0:rows] = high
            at[at_row : at_row + rows, rows : 2 * rows] = (block - high.astype(jnp.float32)).astype(
                jnp.bfloat16
            )

    @pl.when(t == 1)
    def _():
        copy(ls, lb.at[r], LBR, (t, r)).wait_recv()
        spread(lb.at[r], lb.at[r], LB)

    arrived(g0, G0)
    for p in range(parts):
        fill(0, p, g0[p, 0:members])
        fill(1, p, g0[p, members : 2 * members])
    image_f, image_c = product(2)
    own_f, own_c = f_ref[...], c_ref[...]
    image_f = image_f - damp * own_f
    image_c = image_c - damp * own_c
    forcing = lambda p: g0[p, 0:members]
    initial = lambda p: g0[p, members : 2 * members]

    @pl.when(t == 0)
    def _():
        prs[0:members] = image_f
        prs[members : 2 * members] = image_c
        copy(prs, pr.at[r], PRR, (t + 1, r)).start()
        gu[r] = image_c
        spread(gu.at[r], gu.at[r], GU)
        gf[r] = image_f
        spread(gf.at[r], gf.at[r], GF)
        arrived(gu, GU)
        known_c, (t0c, t1c) = second_step(initial, lambda p: gu[p], own_c, image_c)
        arrived(gf, GF)
        known_f, (t0f, t1f) = second_step(forcing, lambda p: gf[p], own_f, image_f)
        tb[r] = packed([t0c, t1c, t0f, t1f, h])
        spread_next(tb.at[r], tp.at[r], TP)
        spread(tb.at[r], tb.at[r], TB)
        arrived(tb, TB)
        t0c, t1c, t0f, t1f = unpacked(tb, 4)
        x1, x2 = start_weights(h, known_c, t0c, t1c)
        x3, x4 = forcing_weights(h, known_f, t0f, t1f)
        o_ref[...] = x1 * own_c + x2 * image_c + (x3 * own_f + x4 * image_f)

    @pl.when(t > 0)
    def _():
        gf[r] = image_f
        spread(gf.at[r], gf.at[r], GF)

        def pass_on():
            copy(prs, pr.at[r], PRR, (t, r)).wait_recv()
            spread(pr.at[r], pr.at[r], PR)

        pl.when(t == 1)(pass_on)
        arrived(gf, GF)
        known_f, (t0f, t1f) = second_step(forcing, lambda p: gf[p], own_f, image_f)
        tf[r] = packed([t0f, t1f])
        spread(tf.at[r], tf.at[r], TF)
        arrived(tf, TF)
        x3, x4 = forcing_weights(h, known_f, *unpacked(tf, 2))
        local = x3 * own_f + x4 * image_f

        @pl.when(t + 1 < slabs)
        def _():
            ls[...] = local
            copy(ls, lb.at[r], LBR, (t + 1, r)).start()

        @pl.when(t > 1)
        def _():
            copy(ls, lb.at[r], LBR, (t, r)).wait_recv()
            spread(lb.at[r], lb.at[r], LB)

        pl.when(t > 1)(pass_on)
        arrived(lb, LB)
        for p in range(parts):
            fill(0, p, lb[p])
        image_l = product(1)[0] - damp * lb[r]
        arrived(pr, PR)
        for p in range(parts):
            fill(0, p, pr[p, 0:members])
            fill(1, p, pr[p, members : 2 * members])
        image_p, image_u = product(2)
        last_p, last_u = pr[r, 0:members], pr[r, members : 2 * members]
        image_p = image_p - damp * last_p
        image_u = image_u - damp * last_u

        early = t == 1
        last_c = lambda p: jnp.where(early, g0[p, members : 2 * members], pr[p, 0:members])
        last_w = lambda p: pr[p, members : 2 * members]
        b2, g = moments(last_c, last_w)
        known_c = (b2, g, jnp.sqrt(remainder(last_c, last_w, g, False) / b2 + EPSILON))
        last_f, last_v = (lambda p: lb[p]), (lambda p: pr[p, 0:members])
        b2, g = moments(last_f, last_v)
        known_l = (b2, g, jnp.sqrt(remainder(last_f, last_v, g, False) / b2 + EPSILON))
        arrived(tp, TP, parts)
        t0c, t1c, t0l, t1l, hs = unpacked(tp, 5)
        hs = hs * (1.0 / parts)
        x1, x2 = start_weights(hs, known_c, t0c, t1c)
        x3, x4 = forcing_weights(hs, known_l, t0l, t1l)
        one = jnp.ones_like(x1)
        e1 = jnp.where(early, x1, 0.0 * one)
        e2 = jnp.where(early, x4, x1)
        e4 = jnp.where(early, x3, one)
        own = e1 * own_c + e2 * last_p + x2 * last_u + e4 * lb[r]
        image = e1 * image_c + e2 * image_p + x2 * image_u + e4 * image_l

        @pl.when(t + 1 < slabs)
        def _():
            prs[0:members] = own
            prs[members : 2 * members] = image
            copy(prs, pr.at[r], PRR, (t + 1, r)).start()

        gu[r] = image
        spread(gu.at[r], gu.at[r], GU)
        for p in range(parts):
            ck[p] = (
                e1 * g0[p, members : 2 * members]
                + e2 * pr[p, 0:members]
                + x2 * pr[p, members : 2 * members]
                + e4 * lb[p]
            )
        arrived(gu, GU)
        known, (t0, t1) = second_step(lambda p: ck[p], lambda p: gu[p], own, image)
        tb[r] = packed([t0, t1, None, None, h])

        @pl.when(t + 1 < slabs)
        def _():
            spread_next(tb.at[r], tp.at[r], TP)

        spread(tb.at[r], tb.at[r], TB)
        arrived(tb, TB)
        x1, x2 = start_weights(h, known, *unpacked(tb, 2))
        o_ref[...] = x1 * own + x2 * image + local

    left(g0, G0)
    left(gf, GF)
    left(gu, GU)
    left(tb, TB)

    @pl.when(t + 1 < slabs)
    def _():
        copy(ls, lb.at[r], LBR, (t, r)).wait_send()
        copy(prs, pr.at[r], PRR, (t, r)).wait_send()
        left(tp, TP, parts)

    @pl.when(t > 0)
    def _():
        left(lb, LB)
        left(pr, PR)
        left(tf, TF)


def on_device(parts, slabs, coupling, damping, forcing, initial, counts):
    members, rows = initial.shape
    whole = coupling.shape[2]
    vmem, ram = pl.BlockSpec(memory_space=pltpu.VMEM), pl.BlockSpec(memory_space=pltpu.SMEM)
    blocks = lambda height: pltpu.VMEM((parts, height, rows), jnp.float32)
    scalars = pltpu.VMEM((parts, 1, LANES), jnp.float32)
    result = pl.pallas_call(
        functools.partial(kernel, members, rows, parts, slabs),
        out_shape=jax.ShapeDtypeStruct((members, rows), jnp.float32),
        in_specs=[pl.BlockSpec(memory_space=pl.ANY), vmem, vmem, vmem, ram],
        out_specs=vmem,
        scratch_shapes=[
            pltpu.VMEM((CHUNKS, rows, whole // CHUNKS), jnp.float32),
            pltpu.VMEM((whole, 2 * rows), jnp.bfloat16),
            pltpu.VMEM((4 * members, whole), jnp.bfloat16),
            blocks(2 * members), blocks(members), blocks(members), blocks(members),
            blocks(2 * members), blocks(members), scalars, scalars, scalars,
            pltpu.VMEM((members, rows), jnp.float32),
            pltpu.VMEM((2 * members, rows), jnp.float32),
            pltpu.SemaphoreType.DMA((CHUNKS,)),
            pltpu.SemaphoreType.DMA((10,)),
            pltpu.SemaphoreType.DMA((10,)),
        ],
        compiler_params=pltpu.CompilerParams(
            collective_id=0, has_side_effects=True, vmem_limit_bytes=40 << 20
        ),
    )(coupling, damping, forcing[0], initial, counts)
    return result[None]


def solution(mesh):
    placed = (P("tm", "row", None), P("tm", "row"), P("tm", None, "row"), P(None, "row"), P("tm"))
    step = functools.partial(on_device, mesh.shape["row"], mesh.shape["tm"])
    return jax.shard_map(
        step, mesh=mesh, in_specs=placed, out_specs=P("tm", None, "row"), check_vma=False
    )
```

time: 361 us -> 81.4 us (0.23); the launches traced: 355 us -> 81.1 us
  matrix products: 156 us -> 0 us
  waiting for transfers between devices: 97.7 us -> 0 us
  Pallas kernels: 0 us -> 74.4 us
  starting transfers between devices: 37 us -> 0 us
  blocking collectives: 26.3 us -> 0 us
  other arithmetic: 15.4 us -> 0 us
  local copies, waits for them, and re-layouts: 20.1 us -> 6.05 us
    dot_general x110 -> x0, matrix products: 156 us -> none  [the longest x8 71.8 us: rows_product(): lax.dot_general(vectors, local_coupling, (((1,), (1,)), ((), ())), precis...]
    pallas_call x0 -> x1, Pallas kernels: none -> 74.4 us  [on_device(): pl.pallas_call(functools.partial(kernel, members, rows, parts, slabs), ou...]
    all_to_all x8 -> x0, waiting for transfers between devices: 70.9 us -> none  [from_everyone(): lax.all_to_all(jnp.broadcast_to(array[None], (size, *array.shape)), axis,...]
    all_to_all x8 -> x0, starting transfers between devices: 33.1 us -> none  [from_everyone(): lax.all_to_all(jnp.broadcast_to(array[None], (size, *array.shape)), axis,...]
    ppermute x3 -> x0, waiting for transfers between devices: 26.9 us -> none  [passed_along(): return lax.ppermute(array, axis, pairs)]
    all_gather x1 -> x0, blocking collectives: 26.3 us -> none  [side_by_side(): lax.all_gather(both, axis, axis=dim, tiled=True)]
    another operation x6 -> x0, other arithmetic: 8.32 us -> none
    scatter x22 -> x0, local copies, waits for them, and re-layouts: 7.72 us -> none  [the longest x5 6.59 us: exponent_block(): augmented = augmented.at[:, 0, KRYLOV].set(1.0)]
  transfers between devices with their start and end apart: 11 -> 0, of which waited for: 11 -> 0; matrix products, arithmetic and copies ran while one was open for 2% -> 0% of each run, Pallas kernels for 0% -> 0%
where the time goes in v1:
time: 81.4 us; the launch traced here: 81.1 us
  Pallas kernels  74.4 us (91%)
  local copies, waits for them, and re-layouts  6.05 us (7%)
    pallas_call x1, Pallas kernels, on_device(): pl.pallas_call(functools.partial(kernel, members, rows, parts, slabs), ou...  74.4 us
    unnamed x9, local copies, waits for them, and re-layouts  6.05 us

profile of v1, /device:TPU:6, one launch (start us, length us, event | category | flops | bytes accessed | tf_op | source)
XLA Modules:
  0.0 81.1 jit_solution(6643649249549572060)
XLA Ops:
  0.7 0.0 copy-start
  0.7 3.4 %copy-done = f32[1,256,8192]{2,1,0:T(8,128)S(1)} copy-done((f32[1,256,8192]{2,1,0:T(8,128)S(1)}, f32[1,256,8192]{2,1,0:T(8,128)}, u32[]{:S(2)}) %copy-start) | copy-done | bytes 8388632
  4.0 0.0 copy-start.1
  4.0 0.7 copy-done.1
  4.7 0.0 copy-start.2
  4.7 0.7 copy-done.2
  5.4 0.0 copy-start.3
  5.4 0.7 copy-done.3
  6.1 74.4 %shard_map.55 = f32[8,256]{1,0:T(8,128)S(1)} custom-call(f32[1,256,8192]{2,1,0:T(8,128)S(1)} %copy-done, f32[1,256]{1,0:T(1,128)S(1)} %copy-done.3, f32[8,256]{1,0:T(8,128)S(1)} %bitcast.3, f32[8,256]{1,0:T(8,128)S(1)} %copy-done.2, s32[1]{0:T(128)S(6)} %copy.7.n_ref), custom_call_target="tpu_custom_call" | custom-call | tf_op jit(solution)/shard_map/pallas_call | solution.py:370
  80.5 0.6 copy.8
Async XLA Ops:
  0.7 3.4 %copy-start = (f32[1,256,8192]{2,1,0:T(8,128)S(1)}, f32[1,256,8192]{2,1,0:T(8,128)}, u32[]{:S(2)}) copy-start(f32[1,256,8192]{2,1,0:T(8,128)} %a_hbm.1) | copy-start | bytes 25165828
  4.0 0.7 copy-start.1
  4.7 0.7 copy-start.2
  5.4 0.7 copy-start.3

commit v2 on v1

v2 whole, which is shorter than its diff:
```python
import functools

import jax
import jax.numpy as jnp
from jax import lax
from jax.experimental import pallas as pl
from jax.experimental.pallas import tpu as pltpu
from jax.sharding import PartitionSpec as P

MESH = pl.DeviceIdType.MESH
TIME_STEP = 0.125
EPSILON = 1e-06
SQUARINGS = 5
TAYLOR_TERMS = 12
SIDE = 4
LANES = 128
CHUNKS = 8


def steps():
    hops = lambda d: min(d, SIDE - d)
    chips = [(z, y) for z in range(SIDE) for y in range(SIDE)]
    chips.sort(key=lambda s: (-hops(s[0]) - hops(s[1]), -abs(hops(s[0]) - hops(s[1]))))
    found = [(hops(z) + hops(y), z, y, flip) for z, y in chips for flip in (0, 1)]
    return found[:-2] + [found[-1], found[-2]]


STEPS = steps()
GROUPS = ((0, 10), (10, 22), (22, 32))


def exponential(h, g, below, above, corner):
    scale = h * (1.0 / 2.0**SQUARINGS)
    s00, s01, s10, s11 = g * scale, above * scale, below * scale, corner * scale
    edge = 1.0 / 2.0**SQUARINGS
    one, zero = jnp.ones_like(s00), jnp.zeros_like(s00)
    r00, r01, r10, r11, c0, c1 = one, zero, zero, one, zero, zero
    for degree in range(TAYLOR_TERMS, 0, -1):
        f = 1.0 / degree
        r00, r01, r10, r11, c0, c1 = (
            1.0 + (s00 * r00 + s01 * r10) * f,
            (s00 * r01 + s01 * r11) * f,
            (s10 * r00 + s11 * r10) * f,
            1.0 + (s10 * r01 + s11 * r11) * f,
            (s00 * c0 + s01 * c1 + edge) * f,
            (s10 * c0 + s11 * c1) * f,
        )
    for _ in range(SQUARINGS):
        r00, r01, r10, r11, c0, c1 = (
            r00 * r00 + r01 * r10,
            r00 * r01 + r01 * r11,
            r10 * r00 + r11 * r10,
            r10 * r01 + r11 * r11,
            r00 * c0 + r01 * c1 + c0,
            r10 * c0 + r11 * c1 + c1,
        )
    return r00, r10, c0, c1


def kernel(
    members, rows, parts, slabs,
    a_hbm, damp_hbm, f_hbm, c_hbm, n_ref, o_ref,
    stage, at, xs, cb, fb, lb, pu, pa, gf, gu, ck, tb, tf, tp, ls, damp_ref,
    a_sem, small_sem, ready, send, recv, recv_one,
):
    t, r = lax.axis_index("tm"), lax.axis_index("row")
    core, chip = lax.rem(r, 2), r // 2
    z, y = chip // SIDE, lax.rem(chip, SIDE)
    zs = [lax.rem(z + d, SIDE) * (2 * SIDE) for d in range(SIDE)]
    ys = [lax.rem(y + d, SIDE) * 2 for d in range(SIDE)]
    cores = (core, 1 - core)
    width = a_hbm.shape[2] // CHUNKS
    C, F, LB, PU, PA, GF, GU, LBR, PUR, PAR, TF, TB, TP = range(13)
    last = parts - 1

    def loads(j):
        return pltpu.make_async_copy(
            a_hbm.at[0, :, pl.ds(j * width, width)], stage.at[:, pl.ds(j * width, width)], a_sem.at[j]
        )

    small = [
        pltpu.make_async_copy(from_ref, to_ref, small_sem.at[i])
        for i, (from_ref, to_ref) in enumerate(
            ((f_hbm, fb.at[last]), (c_hbm, cb.at[last]), (damp_hbm, damp_ref))
        )
    ]

    def copy(src, dst, k, arrival, device):
        return pltpu.make_async_remote_copy(
            src_ref=src, dst_ref=dst, send_sem=send.at[k], recv_sem=arrival,
            device_id=device, device_id_type=MESH,
        )

    def relay(src, dst, k):
        return copy(src, dst.at[last], k, recv_one.at[k], (t + 1, r))

    def spread(buffer, k):
        for group, (low, high) in enumerate(GROUPS):
            for i in range(low, min(high, last)):
                _, dz, dy, flip = STEPS[i]
                copy(
                    buffer.at[last], buffer.at[i], k, recv.at[k, group], (t, zs[dz] + ys[dy] + cores[flip])
                ).start()

    def spread_sums(buffer, k):
        for i in range(last):
            _, dz, dy, flip = STEPS[i]
            copy(
                buffer.at[last], buffer.at[i], k, recv_one.at[k], (t, zs[dz] + ys[dy] + cores[flip])
            ).start()

    def spread_next():
        for _, dz, dy, flip in STEPS:
            i = STEPS.index((_, dz, dy, flip))
            copy(
                tb.at[last], tp.at[i], TP, recv_one.at[TP], (t + 1, zs[dz] + ys[dy] + cores[flip])
            ).start()

    def arrived(buffer, k, group):
        low, high = GROUPS[group]
        some = buffer.at[pl.ds(0, min(high, last) - low)]
        pltpu.make_async_copy(some, some, recv.at[k, group]).wait()

    def took(buffer, semaphore, count):
        some = buffer.at[pl.ds(0, count)]
        pltpu.make_async_copy(some, some, semaphore).wait()

    def fill(at_part, v):
        high = v.astype(jnp.bfloat16).astype(jnp.float32)
        both = jnp.concatenate([high, v - high], axis=0).astype(jnp.bfloat16)
        xs[:, rows * at_part : rows * at_part + rows] = both

    def applied(buffer, k, beside=None):
        total = jnp.zeros((2 * members, 2 * rows), jnp.float32)
        n2 = jnp.zeros((members, rows), jnp.float32)
        d = jnp.zeros((members, rows), jnp.float32)
        if beside is not None:
            for p in range(parts):
                n2 += beside[p] * beside[p]
            b2 = jnp.sum(n2, axis=1, keepdims=True) + EPSILON
        for group, (low, high) in enumerate(GROUPS):
            arrived(buffer, k, group)
            for p in range(low, high):
                v = buffer[p]
                fill(p, v)
                if beside is not None:
                    d += beside[p] * v
            total += jnp.dot(
                xs[:, rows * low : rows * high], at[rows * low : rows * high, :],
                preferred_element_type=jnp.float32,
            )
        top, under = total[:members], total[members:]
        image = top[:, :rows] + (top[:, rows:] + under[:, :rows]) - damp * buffer[last]
        if beside is None:
            return image
        return image, b2, jnp.sum(d, axis=1, keepdims=True) / b2

    def below(first, second, b2, g):
        w2 = jnp.zeros((members, rows), jnp.float32)
        for p in range(parts):
            w = second[p] - g * first[p]
            w2 += w * w
        return jnp.sqrt(jnp.sum(w2, axis=1, keepdims=True) / b2 + EPSILON)

    def sums(first, second, image, g):
        w = second - g * first
        image = image - g * second
        return (
            jnp.sum(first * image, axis=1, keepdims=True),
            jnp.sum(w * image, axis=1, keepdims=True),
        )

    lane = lax.broadcasted_iota(jnp.int32, (members, LANES), 1)
    member = lax.broadcasted_iota(jnp.int32, (members, LANES), 0)

    def packed(columns):
        row = jnp.zeros((members, LANES), jnp.float32)
        for j, column in enumerate(columns):
            if column is not None:
                row = jnp.where(lane == member + members * j, column, row)
        return jnp.sum(row, axis=0, keepdims=True)

    def unpacked(buffer, count):
        total = jnp.sum(buffer[...], axis=0)
        total = jnp.broadcast_to(total, (members, LANES))
        return [
            jnp.sum(jnp.where(lane == member + members * j, total, 0.0), axis=1, keepdims=True)
            for j in range(count)
        ]

    def start_weights(h, known, t0, t1):
        b2, g, side = known
        e00, e10, _, _ = exponential(h, g, side, t0 / (b2 * side), t1 / (b2 * side * side))
        x2 = e10 / side
        return e00 - g * x2, x2

    def forcing_weights(h, known, t0, t1):
        b2, g, side = known
        _, _, c0, c1 = exponential(h, g, side, t0 / (b2 * side), t1 / (b2 * side * side))
        x4 = h * c1 / side
        return h * c0 - g * x4, x4

    for copy_in in small:
        copy_in.start()
    for j in range(CHUNKS):
        loads(j).start()

    barrier = pltpu.get_barrier_semaphore()
    for _, dz, dy, flip in STEPS[:-1]:
        pl.semaphore_signal(
            barrier, inc=1, device_id=(t, zs[dz] + ys[dy] + cores[flip]), device_id_type=MESH
        )

    @pl.when(t > 0)
    def _():
        pl.semaphore_signal(barrier, inc=1, device_id=(t - 1, r), device_id_type=MESH)

    @pl.when(t + 1 < slabs)
    def _():
        pl.semaphore_signal(barrier, inc=1, device_id=(t + 1, r), device_id_type=MESH)

    for copy_in in small:
        copy_in.wait()
    h = jnp.full((members, 1), n_ref[0].astype(jnp.float32) * TIME_STEP, jnp.float32)
    damp = damp_ref[...]
    pl.semaphore_wait(barrier, last + jnp.minimum(t, 1) + jnp.minimum(slabs - 1 - t, 1))

    @pl.when(t > 0)
    def _():
        pl.semaphore_signal(ready, inc=1, device_id=(t - 1, r), device_id_type=MESH)

    @pl.when(t == 0)
    def _():
        relay(fb.at[last], lb, LBR).start()
        spread(cb, C)

    spread(fb, F)

    @pl.when(t == 1)
    def _():
        spread(cb, C)

    for j in range(CHUNKS):
        loads(j).wait()
    for i, (_, dz, dy, flip) in enumerate(STEPS):
        source = zs[(SIDE - dz) % SIDE] + ys[(SIDE - dy) % SIDE] + cores[flip]
        block = stage[:, pl.ds(pl.multiple_of(source * rows, rows), rows)].T
        high = block.astype(jnp.bfloat16)
        at[i * rows : (i + 1) * rows, 0:rows] = high
        at[i * rows : (i + 1) * rows, rows : 2 * rows] = (block - high.astype(jnp.float32)).astype(
            jnp.bfloat16
        )

    own_f = fb[last]

    @pl.when(t == 0)
    def _():
        own_c = cb[last]
        image_c = applied(cb, C)
        gu[last] = image_c
        relay(gu.at[last], pu, PUR).start()
        spread(gu, GU)
        image_f = applied(fb, F)
        gf[last] = image_f
        relay(gf.at[last], pa, PAR).start()
        spread(gf, GF)
        image, b2, g = applied(gu, GU, cb)
        t0c, t1c = sums(own_c, image_c, image, g)
        known_c = (b2, g, below(cb, gu, b2, g))
        image, b2, g = applied(gf, GF, fb)
        t0f, t1f = sums(own_f, image_f, image, g)
        tb[last] = packed([t0c, t1c, t0f, t1f, h])
        pl.semaphore_wait(ready, 1)
        spread_next()
        spread_sums(tb, TB)
        known_f = (b2, g, below(fb, gf, b2, g))
        took(tb, recv_one.at[TB], last)
        t0c, t1c, t0f, t1f = unpacked(tb, 4)
        x1, x2 = start_weights(h, known_c, t0c, t1c)
        x3, x4 = forcing_weights(h, known_f, t0f, t1f)
        o_ref[...] = x1 * own_c + x2 * image_c + (x3 * own_f + x4 * image_f)

    def later(early):
        def pass_on(buffer, one, k):
            copy(ls, buffer.at[last], k, recv_one.at[one], (t, r)).wait_recv()
            spread(buffer, k)

        if early:
            pass_on(lb, LBR, LB)
        image_f = applied(fb, F)
        gf[last] = image_f
        spread(gf, GF)
        if early:
            image_c = applied(cb, C)
            pass_on(pu, PUR, PU)
            pass_on(pa, PAR, PA)
            image_l = applied(lb, LB)
        image, b2, g = applied(gf, GF, fb)
        tf[last] = packed(list(sums(own_f, image_f, image, g)))
        spread_sums(tf, TF)
        known_f = (b2, g, below(fb, gf, b2, g))

        def finish_forcing():
            took(tf, recv_one.at[TF], last)
            x3, x4 = forcing_weights(h, known_f, *unpacked(tf, 2))
            local = x3 * own_f + x4 * image_f

            @pl.when(t + 1 < slabs)
            def _():
                ls[...] = local
                copy(ls, lb.at[last], LBR, recv_one.at[LBR], (t + 1, r)).start()

            return local

        if early:
            image_u, b2c, gc = applied(pu, PU, cb)
            known_c = (b2c, gc, below(cb, pu, b2c, gc))
            image_p, b2l, gl = applied(pa, PA, lb)
            known_l = (b2l, gl, below(lb, pa, b2l, gl))
            local = finish_forcing()
        else:
            local = finish_forcing()
            pass_on(lb, LBR, LB)
            pass_on(pu, PUR, PU)
            pass_on(pa, PAR, PA)
            image_l = applied(lb, LB)
            image_u = applied(pu, PU)
            image_p, b2c, gc = applied(pa, PA, pu)
            n2 = jnp.zeros((members, rows), jnp.float32)
            for p in range(parts):
                n2 += pa[p] * pa[p]
            b2u = b2c
            b2c = jnp.sum(n2, axis=1, keepdims=True) + EPSILON
            gc = gc * b2u / b2c
            known_c = (b2c, gc, below(pa, pu, b2c, gc))
        took(tp, recv_one.at[TP], parts)
        t0c, t1c, t0l, t1l, hs = unpacked(tp, 5)
        hs = hs * (1.0 / parts)
        x1, x2 = start_weights(hs, known_c, t0c, t1c)
        if early:
            x3, x4 = forcing_weights(hs, known_l, t0l, t1l)
            state = lambda p: x1 * cb[p] + x2 * pu[p] + (x3 * lb[p] + x4 * pa[p])
            image = x1 * image_c + x2 * image_u + (x3 * image_l + x4 * image_p)
        else:
            state = lambda p: x1 * pa[p] + x2 * pu[p] + lb[p]
            image = x1 * image_p + x2 * image_u + image_l
        gu[last] = image
        ck[last] = state(last)

        @pl.when(t + 1 < slabs)
        def _():
            relay(gu.at[last], pu, PUR).start()
            relay(ck.at[last], pa, PAR).start()

        spread(gu, GU)
        for p in range(last):
            ck[p] = state(p)
        own = ck[last]
        again, b2, g = applied(gu, GU, ck)
        tb[last] = packed([*sums(own, image, again, g), None, None, h])

        @pl.when(t + 1 < slabs)
        def _():
            pl.semaphore_wait(ready, 1)
            spread_next()

        spread_sums(tb, TB)
        known = (b2, g, below(ck, gu, b2, g))
        took(tb, recv_one.at[TB], last)
        x1, x2 = start_weights(h, known, *unpacked(tb, 2))
        o_ref[...] = x1 * own + x2 * image + local

    pl.when(t == 1)(functools.partial(later, True))
    pl.when(t > 1)(functools.partial(later, False))

    for buffer, k in ((fb, F), (gf, GF), (gu, GU), (tb, TB)):
        took(buffer, send.at[k], last)

    @pl.when(t < 2)
    def _():
        took(cb, send.at[C], last)

    @pl.when(t + 1 < slabs)
    def _():
        for k in (LBR, PUR, PAR):
            took(lb, send.at[k], 1)
        took(tp, send.at[TP], parts)

    @pl.when(t > 0)
    def _():
        for buffer, k in ((lb, LB), (pu, PU), (pa, PA), (tf, TF)):
            took(buffer, send.at[k], last)


def on_device(parts, slabs, coupling, damping, forcing, initial, counts):
    members, rows = initial.shape
    whole = coupling.shape[2]
    far, ram = pl.BlockSpec(memory_space=pl.ANY), pl.BlockSpec(memory_space=pltpu.SMEM)
    blocks = pltpu.VMEM((parts, members, rows), jnp.float32)
    scalars = pltpu.VMEM((parts, 1, LANES), jnp.float32)
    result = pl.pallas_call(
        functools.partial(kernel, members, rows, parts, slabs),
        out_shape=jax.ShapeDtypeStruct((members, rows), jnp.float32),
        in_specs=[far, far, far, far, ram],
        out_specs=pl.BlockSpec(memory_space=pltpu.VMEM),
        scratch_shapes=[
            pltpu.VMEM((rows, whole), jnp.float32),
            pltpu.VMEM((whole, 2 * rows), jnp.bfloat16),
            pltpu.VMEM((2 * members, whole), jnp.bfloat16),
            *[blocks] * 8,
            *[scalars] * 3,
            pltpu.VMEM((members, rows), jnp.float32),
            pltpu.VMEM((1, rows), jnp.float32),
            pltpu.SemaphoreType.DMA((CHUNKS,)),
            pltpu.SemaphoreType.DMA((3,)),
            pltpu.SemaphoreType.REGULAR,
            pltpu.SemaphoreType.DMA((13,)),
            pltpu.SemaphoreType.DMA((7, len(GROUPS))),
            pltpu.SemaphoreType.DMA((13,)),
        ],
        compiler_params=pltpu.CompilerParams(
            collective_id=0, has_side_effects=True, vmem_limit_bytes=60 << 20
        ),
    )(coupling, damping, forcing[0], initial, counts)
    return result[None]


def solution(mesh):
    placed = (P("tm", "row", None), P("tm", "row"), P("tm", None, "row"), P(None, "row"), P("tm"))
    step = functools.partial(on_device, mesh.shape["row"], mesh.shape["tm"])
    return jax.shard_map(
        step, mesh=mesh, in_specs=placed, out_specs=P("tm", None, "row"), check_vma=False
    )
```

time: 81.4 us -> 69.8 us (0.86)
  Pallas kernels: 74.4 us -> 67.7 us
  local copies, waits for them, and re-layouts: 6.05 us -> 1.3 us
    pallas_call x1, Pallas kernels: 74.4 us -> 67.7 us  [on_device(): pl.pallas_call(functools.partial(kernel, members, rows, parts, slabs), ou...]
    unnamed x9 -> x1, local copies, waits for them, and re-layouts: 6.05 us -> 1.3 us
where the time goes in v2:
time: 69.8 us; the launch traced here: 69.7 us
  Pallas kernels  67.7 us (97%)
  local copies, waits for them, and re-layouts  1.3 us (2%)
    pallas_call x1, Pallas kernels, on_device(): pl.pallas_call(functools.partial(kernel, members, rows, parts, slabs), ou...  67.7 us

profile of v2, /device:TPU:6, one launch (start us, length us, event | category | flops | bytes accessed | tf_op | source)
XLA Modules:
  0.0 69.7 jit_solution(16871366859396915710)
XLA Ops:
  0.7 67.7 %shard_map.55 = f32[8,256]{1,0:T(8,128)} custom-call(f32[1,256,8192]{2,1,0:T(8,128)} %a_hbm.1, f32[1,256]{1,0:T(1,128)} %damp_hbm.1, f32[8,256]{1,0:T(8,128)} %bitcast.3, f32[8,256]{1,0:T(8,128)} %c_hbm.1, s32[1]{0:T(128)S(6)} %copy.7.n_ref), custom_call_target="tpu_custom_call" | custom-call | tf_op jit(solution)/shard_map/pallas_call | solution.py:401
  68.4 1.3 %copy.8 = f32[1,8,256]{2,1,0:T(8,128)} copy(f32[1,8,256]{2,1,0:T(8,128)} %bitcast.2) | data formatting | bytes 16384

commit v3 on v2

--- a/solution.py
+++ b/solution.py
@@ -21,12 +21,14 @@
     hops = lambda d: min(d, SIDE - d)
     chips = [(z, y) for z in range(SIDE) for y in range(SIDE)]
     chips.sort(key=lambda s: (-hops(s[0]) - hops(s[1]), -abs(hops(s[0]) - hops(s[1]))))
-    found = [(hops(z) + hops(y), z, y, flip) for z, y in chips for flip in (0, 1)]
-    return found[:-2] + [found[-1], found[-2]]
+    return [(z, y, flip) for flip in (0, 1) for z, y in chips]
 
 
 STEPS = steps()
-GROUPS = ((0, 10), (10, 22), (22, 32))
+CHIPS = len(STEPS) // 2
+OWN = CHIPS - 1
+GROUPS = ((0, 5), (5, 11), (11, 15))
+BY_DISTANCE = [i + CHIPS * flip for i in range(CHIPS) for flip in (0, 1)]
 
 
 def exponential(h, g, below, above, corner):
@@ -81,7 +83,7 @@
     small = [
         pltpu.make_async_copy(from_ref, to_ref, small_sem.at[i])
         for i, (from_ref, to_ref) in enumerate(
-            ((f_hbm, fb.at[last]), (c_hbm, cb.at[last]), (damp_hbm, damp_ref))
+            ((f_hbm, fb.at[OWN]), (c_hbm, cb.at[OWN]), (damp_hbm, damp_ref))
         )
     ]
 
@@ -91,69 +93,87 @@
             device_id=device, device_id_type=MESH,
         )
 
+    def device(i):
+        dz, dy, flip = STEPS[i]
+        return zs[dz] + ys[dy] + cores[flip]
+
     def relay(src, dst, k):
-        return copy(src, dst.at[last], k, recv_one.at[k], (t + 1, r))
+        return copy(src, dst.at[OWN], k, recv_one.at[k], (t + 1, r))
 
     def spread(buffer, k):
+        own = buffer.at[OWN]
         for group, (low, high) in enumerate(GROUPS):
-            for i in range(low, min(high, last)):
-                _, dz, dy, flip = STEPS[i]
-                copy(
-                    buffer.at[last], buffer.at[i], k, recv.at[k, group], (t, zs[dz] + ys[dy] + cores[flip])
-                ).start()
+            for i in range(low, high):
+                copy(own, buffer.at[i], k, recv.at[k, group], (t, device(i))).start()
+        copy(own, buffer.at[last], k, recv.at[k, 2 * len(GROUPS) - 1], (t, device(last))).start()
+
+    def forward(buffer, k):
+        for group, (low, high) in enumerate(GROUPS):
+            took(buffer, recv.at[k, group], high - low)
+            copy(
+                buffer.at[pl.ds(low, high - low)], buffer.at[pl.ds(CHIPS + low, high - low)],
+                k, recv.at[k, len(GROUPS) + group], (t, device(last)),
+            ).start()
 
     def spread_sums(buffer, k):
-        for i in range(last):
-            _, dz, dy, flip = STEPS[i]
-            copy(
-                buffer.at[last], buffer.at[i], k, recv_one.at[k], (t, zs[dz] + ys[dy] + cores[flip])
-            ).start()
+        for i in BY_DISTANCE:
+            if i != OWN:
+                copy(buffer.at[OWN], buffer.at[i], k, recv_one.at[k], (t, device(i))).start()
 
     def spread_next():
-        for _, dz, dy, flip in STEPS:
-            i = STEPS.index((_, dz, dy, flip))
-            copy(
-                tb.at[last], tp.at[i], TP, recv_one.at[TP], (t + 1, zs[dz] + ys[dy] + cores[flip])
-            ).start()
-
-    def arrived(buffer, k, group):
-        low, high = GROUPS[group]
-        some = buffer.at[pl.ds(0, min(high, last) - low)]
-        pltpu.make_async_copy(some, some, recv.at[k, group]).wait()
+        for i in BY_DISTANCE:
+            copy(tb.at[OWN], tp.at[i], TP, recv_one.at[TP], (t + 1, device(i))).start()
 
     def took(buffer, semaphore, count):
         some = buffer.at[pl.ds(0, count)]
         pltpu.make_async_copy(some, some, semaphore).wait()
 
-    def fill(at_part, v):
+    def fill(slot, at_part, v):
         high = v.astype(jnp.bfloat16).astype(jnp.float32)
         both = jnp.concatenate([high, v - high], axis=0).astype(jnp.bfloat16)
-        xs[:, rows * at_part : rows * at_part + rows] = both
-
-    def applied(buffer, k, beside=None):
-        total = jnp.zeros((2 * members, 2 * rows), jnp.float32)
-        n2 = jnp.zeros((members, rows), jnp.float32)
-        d = jnp.zeros((members, rows), jnp.float32)
-        if beside is not None:
-            for p in range(parts):
-                n2 += beside[p] * beside[p]
-            b2 = jnp.sum(n2, axis=1, keepdims=True) + EPSILON
-        for group, (low, high) in enumerate(GROUPS):
-            arrived(buffer, k, group)
-            for p in range(low, high):
-                v = buffer[p]
-                fill(p, v)
-                if beside is not None:
-                    d += beside[p] * v
+        xs[16 * slot : 16 * slot + 16, rows * at_part : rows * at_part + rows] = both
+
+    def applied(*gathers):
+        count = len(gathers)
+        total = jnp.zeros((2 * members * count, 2 * rows), jnp.float32)
+        norms, d = {}, {}
+        for j, (buffer, k, *beside) in enumerate(gathers):
+            forward(buffer, k)
+            if beside:
+                n2 = jnp.zeros((members, rows), jnp.float32)
+                d[j] = jnp.zeros((members, rows), jnp.float32)
+                if not any(beside[0] is earlier[0] for earlier in gathers):
+                    for p in range(parts):
+                        n2 += beside[0][p] * beside[0][p]
+                norms[j] = n2
+        ends = [0, CHIPS, *(CHIPS + high for _, high in GROUPS[:-1]), parts]
+        for group, (low, high) in enumerate(zip(ends, ends[1:])):
+            for j, (buffer, k, *_) in enumerate(gathers):
+                if group > 0:
+                    took(buffer, recv.at[k, len(GROUPS) + group - 1], high - low)
+                for p in range(low, high):
+                    fill(j, p, buffer[p])
+            for j, (buffer, _, *beside) in enumerate(gathers):
+                if beside:
+                    for p in range(low, high):
+                        d[j] += beside[0][p] * buffer[p]
+                        if any(beside[0] is earlier[0] for earlier in gathers):
+                            norms[j] += beside[0][p] * beside[0][p]
             total += jnp.dot(
-                xs[:, rows * low : rows * high], at[rows * low : rows * high, :],
+                xs[0 : 16 * count, rows * low : rows * high], at[rows * low : rows * high, :],
                 preferred_element_type=jnp.float32,
             )
-        top, under = total[:members], total[members:]
-        image = top[:, :rows] + (top[:, rows:] + under[:, :rows]) - damp * buffer[last]
-        if beside is None:
-            return image
-        return image, b2, jnp.sum(d, axis=1, keepdims=True) / b2
+        out = []
+        for j, (buffer, _, *beside) in enumerate(gathers):
+            at_row = 2 * members * j
+            top, under = total[at_row : at_row + members], total[at_row + members : at_row + 2 * members]
+            image = top[:, :rows] + (top[:, rows:] + under[:, :rows]) - damp * buffer[OWN]
+            if beside:
+                b2 = jnp.sum(norms[j], axis=1, keepdims=True) + EPSILON
+                out.append((image, b2, jnp.sum(d[j], axis=1, keepdims=True) / b2))
+            else:
+                out.append(image)
+        return out[0] if count == 1 else out
 
     def below(first, second, b2, g):
         w2 = jnp.zeros((members, rows), jnp.float32)
@@ -206,10 +226,8 @@
         loads(j).start()
 
     barrier = pltpu.get_barrier_semaphore()
-    for _, dz, dy, flip in STEPS[:-1]:
-        pl.semaphore_signal(
-            barrier, inc=1, device_id=(t, zs[dz] + ys[dy] + cores[flip]), device_id_type=MESH
-        )
+    for i in (*range(OWN), last):
+        pl.semaphore_signal(barrier, inc=1, device_id=(t, device(i)), device_id_type=MESH)
 
     @pl.when(t > 0)
     def _():
@@ -223,15 +241,11 @@
         copy_in.wait()
     h = jnp.full((members, 1), n_ref[0].astype(jnp.float32) * TIME_STEP, jnp.float32)
     damp = damp_ref[...]
-    pl.semaphore_wait(barrier, last + jnp.minimum(t, 1) + jnp.minimum(slabs - 1 - t, 1))
-
-    @pl.when(t > 0)
-    def _():
-        pl.semaphore_signal(ready, inc=1, device_id=(t - 1, r), device_id_type=MESH)
+    pl.semaphore_wait(barrier, CHIPS + jnp.minimum(t, 1) + jnp.minimum(slabs - 1 - t, 1))
 
     @pl.when(t == 0)
     def _():
-        relay(fb.at[last], lb, LBR).start()
+        relay(fb.at[OWN], lb, LBR).start()
         spread(cb, C)
 
     spread(fb, F)
@@ -242,7 +256,7 @@
 
     for j in range(CHUNKS):
         loads(j).wait()
-    for i, (_, dz, dy, flip) in enumerate(STEPS):
+    for i, (dz, dy, flip) in enumerate(STEPS):
         source = zs[(SIDE - dz) % SIDE] + ys[(SIDE - dy) % SIDE] + cores[flip]
         block = stage[:, pl.ds(pl.multiple_of(source * rows, rows), rows)].T
         high = block.astype(jnp.bfloat16)
@@ -251,25 +265,25 @@
             jnp.bfloat16
         )
 
-    own_f = fb[last]
+    own_f = fb[OWN]
 
     @pl.when(t == 0)
     def _():
-        own_c = cb[last]
-        image_c = applied(cb, C)
-        gu[last] = image_c
-        relay(gu.at[last], pu, PUR).start()
+        own_c = cb[OWN]
+        image_c = applied((cb, C))
+        gu[OWN] = image_c
+        relay(gu.at[OWN], pu, PUR).start()
         spread(gu, GU)
-        image_f = applied(fb, F)
-        gf[last] = image_f
-        relay(gf.at[last], pa, PAR).start()
+        image_f = applied((fb, F))
+        gf[OWN] = image_f
+        relay(gf.at[OWN], pa, PAR).start()
         spread(gf, GF)
-        image, b2, g = applied(gu, GU, cb)
+        image, b2, g = applied((gu, GU, cb))
         t0c, t1c = sums(own_c, image_c, image, g)
         known_c = (b2, g, below(cb, gu, b2, g))
-        image, b2, g = applied(gf, GF, fb)
+        image, b2, g = applied((gf, GF, fb))
         t0f, t1f = sums(own_f, image_f, image, g)
-        tb[last] = packed([t0c, t1c, t0f, t1f, h])
+        tb[OWN] = packed([t0c, t1c, t0f, t1f, h])
         pl.semaphore_wait(ready, 1)
         spread_next()
         spread_sums(tb, TB)
@@ -282,21 +296,21 @@
 
     def later(early):
         def pass_on(buffer, one, k):
-            copy(ls, buffer.at[last], k, recv_one.at[one], (t, r)).wait_recv()
+            copy(ls, buffer.at[OWN], k, recv_one.at[one], (t, r)).wait_recv()
             spread(buffer, k)
 
         if early:
             pass_on(lb, LBR, LB)
-        image_f = applied(fb, F)
-        gf[last] = image_f
+        image_f = applied((fb, F))
+        pl.semaphore_signal(ready, inc=1, device_id=(t - 1, r), device_id_type=MESH)
+        gf[OWN] = image_f
         spread(gf, GF)
         if early:
-            image_c = applied(cb, C)
+            image_c = applied((cb, C))
             pass_on(pu, PUR, PU)
             pass_on(pa, PAR, PA)
-            image_l = applied(lb, LB)
-        image, b2, g = applied(gf, GF, fb)
-        tf[last] = packed(list(sums(own_f, image_f, image, g)))
+        image, b2, g = applied((gf, GF, fb))
+        tf[OWN] = packed(list(sums(own_f, image_f, image, g)))
         spread_sums(tf, TF)
         known_f = (b2, g, below(fb, gf, b2, g))
 
@@ -308,14 +322,14 @@
             @pl.when(t + 1 < slabs)
             def _():
                 ls[...] = local
-                copy(ls, lb.at[last], LBR, recv_one.at[LBR], (t + 1, r)).start()
+                copy(ls, lb.at[OWN], LBR, recv_one.at[LBR], (t + 1, r)).start()
 
             return local
 
         if early:
-            image_u, b2c, gc = applied(pu, PU, cb)
+            image_l = applied((lb, LB))
+            (image_u, b2c, gc), (image_p, b2l, gl) = applied((pu, PU, cb), (pa, PA, lb))
             known_c = (b2c, gc, below(cb, pu, b2c, gc))
-            image_p, b2l, gl = applied(pa, PA, lb)
             known_l = (b2l, gl, below(lb, pa, b2l, gl))
             local = finish_forcing()
         else:
@@ -323,15 +337,7 @@
             pass_on(lb, LBR, LB)
             pass_on(pu, PUR, PU)
             pass_on(pa, PAR, PA)
-            image_l = applied(lb, LB)
-            image_u = applied(pu, PU)
-            image_p, b2c, gc = applied(pa, PA, pu)
-            n2 = jnp.zeros((members, rows), jnp.float32)
-            for p in range(parts):
-                n2 += pa[p] * pa[p]
-            b2u = b2c
-            b2c = jnp.sum(n2, axis=1, keepdims=True) + EPSILON
-            gc = gc * b2u / b2c
+            image_l, image_p, (image_u, b2c, gc) = applied((lb, LB), (pa, PA), (pu, PU, pa))
             known_c = (b2c, gc, below(pa, pu, b2c, gc))
         took(tp, recv_one.at[TP], parts)
         t0c, t1c, t0l, t1l, hs = unpacked(tp, 5)
@@ -344,20 +350,21 @@
         else:
             state = lambda p: x1 * pa[p] + x2 * pu[p] + lb[p]
             image = x1 * image_p + x2 * image_u + image_l
-        gu[last] = image
-        ck[last] = state(last)
+        gu[OWN] = image
+        ck[OWN] = state(OWN)
 
         @pl.when(t + 1 < slabs)
         def _():
-            relay(gu.at[last], pu, PUR).start()
-            relay(ck.at[last], pa, PAR).start()
+            relay(gu.at[OWN], pu, PUR).start()
+            relay(ck.at[OWN], pa, PAR).start()
 
         spread(gu, GU)
-        for p in range(last):
-            ck[p] = state(p)
-        own = ck[last]
-        again, b2, g = applied(gu, GU, ck)
-        tb[last] = packed([*sums(own, image, again, g), None, None, h])
+        for p in range(parts):
+            if p != OWN:
+                ck[p] = state(p)
+        own = ck[OWN]
+        again, b2, g = applied((gu, GU, ck))
+        tb[OWN] = packed([*sums(own, image, again, g), None, None, h])
 
         @pl.when(t + 1 < slabs)
         def _():
@@ -406,7 +413,7 @@
         scratch_shapes=[
             pltpu.VMEM((rows, whole), jnp.float32),
             pltpu.VMEM((whole, 2 * rows), jnp.bfloat16),
-            pltpu.VMEM((2 * members, whole), jnp.bfloat16),
+            pltpu.VMEM((6 * members, whole), jnp.bfloat16),
             *[blocks] * 8,
             *[scalars] * 3,
             pltpu.VMEM((members, rows), jnp.float32),
@@ -415,7 +422,7 @@
             pltpu.SemaphoreType.DMA((3,)),
             pltpu.SemaphoreType.REGULAR,
             pltpu.SemaphoreType.DMA((13,)),
-            pltpu.SemaphoreType.DMA((7, len(GROUPS))),
+            pltpu.SemaphoreType.DMA((7, 2 * len(GROUPS))),
             pltpu.SemaphoreType.DMA((13,)),
         ],
         compiler_params=pltpu.CompilerParams(

time: 69.8 us -> 64.8 us (0.928)
  Pallas kernels: 67.7 us -> 62.6 us
    pallas_call x1, Pallas kernels: 67.7 us -> 62.6 us  [on_device(): pl.pallas_call(functools.partial(kernel, members, rows, parts, slabs), ou...]
where the time goes in v3:
time: 64.8 us; the launch traced here: 64.6 us
  Pallas kernels  62.6 us (97%)
  local copies, waits for them, and re-layouts  1.3 us (2%)
  between operations  0.66 us (1%)
    pallas_call x1, Pallas kernels, on_device(): pl.pallas_call(functools.partial(kernel, members, rows, parts, slabs), ou...  62.6 us
    unnamed x1, local copies, waits for them, and re-layouts  1.3 us

profile of v3, /device:TPU:6, one launch (start us, length us, event | category | flops | bytes accessed | tf_op | source)
XLA Modules:
  0.0 64.6 jit_solution(15939609724904070100)
XLA Ops:
  0.7 62.6 %shard_map.55 = f32[8,256]{1,0:T(8,128)} custom-call(f32[1,256,8192]{2,1,0:T(8,128)} %a_hbm.1, f32[1,256]{1,0:T(1,128)} %damp_hbm.1, f32[8,256]{1,0:T(8,128)} %bitcast.3, f32[8,256]{1,0:T(8,128)} %c_hbm.1, s32[1]{0:T(128)S(6)} %copy.7.n_ref), custom_call_target="tpu_custom_call" | custom-call | tf_op jit(solution)/shard_map/pallas_call | solution.py:408
  63.3 1.3 %copy.8 = f32[1,8,256]{2,1,0:T(8,128)} copy(f32[1,8,256]{2,1,0:T(8,128)} %bitcast.2) | data formatting | bytes 16384

commit v4 on v3

--- a/solution.py
+++ b/solution.py
@@ -1,4 +1,5 @@
 import functools
+import math
 
 import jax
 import jax.numpy as jnp
@@ -14,6 +15,7 @@
 TAYLOR_TERMS = 12
 SIDE = 4
 LANES = 128
+LATE = 4
 CHUNKS = 8
 
 
@@ -27,42 +29,46 @@
 STEPS = steps()
 CHIPS = len(STEPS) // 2
 OWN = CHIPS - 1
-GROUPS = ((0, 5), (5, 11), (11, 15))
+GROUPS = ((0, 3), (3, 6), (6, 9), (9, 12), (12, 15))
 BY_DISTANCE = [i + CHIPS * flip for i in range(CHIPS) for flip in (0, 1)]
 
 
 def exponential(h, g, below, above, corner):
     scale = h * (1.0 / 2.0**SQUARINGS)
-    s00, s01, s10, s11 = g * scale, above * scale, below * scale, corner * scale
+    s = (g * scale, above * scale, below * scale, corner * scale)
+    times = lambda a, b: (
+        a[0] * b[0] + a[1] * b[2], a[0] * b[1] + a[1] * b[3],
+        a[2] * b[0] + a[3] * b[2], a[2] * b[1] + a[3] * b[3],
+    )
+    plus = lambda a, b: tuple(x + y for x, y in zip(a, b))
+    s2 = times(s, s)
+    s3, s4 = times(s2, s), times(s2, s2)
+
+    def four(coefficients):
+        c0, c1, c2, c3 = coefficients
+        out = [(a * c1 + b * c2) + c * c3 for a, b, c in zip(s, s2, s3)]
+        return (out[0] + c0, out[1], out[2], out[3] + c0)
+
+    term = [1.0 / math.factorial(k) for k in range(TAYLOR_TERMS + 1)]
+    r = plus(four(term[8:12]), tuple(x * term[12] for x in s4))
+    r = plus(four(term[4:8]), times(s4, r))
+    r = plus(four(term[0:4]), times(s4, r))
     edge = 1.0 / 2.0**SQUARINGS
-    one, zero = jnp.ones_like(s00), jnp.zeros_like(s00)
-    r00, r01, r10, r11, c0, c1 = one, zero, zero, one, zero, zero
-    for degree in range(TAYLOR_TERMS, 0, -1):
-        f = 1.0 / degree
-        r00, r01, r10, r11, c0, c1 = (
-            1.0 + (s00 * r00 + s01 * r10) * f,
-            (s00 * r01 + s01 * r11) * f,
-            (s10 * r00 + s11 * r10) * f,
-            1.0 + (s10 * r01 + s11 * r11) * f,
-            (s00 * c0 + s01 * c1 + edge) * f,
-            (s10 * c0 + s11 * c1) * f,
-        )
+    first = lambda a: (a[0], a[2])
+    on = lambda a, v: (a[0] * v[0] + a[1] * v[1], a[2] * v[0] + a[3] * v[1])
+    c = first(four(term[9:13]))
+    c = plus(first(four(term[5:9])), on(s4, c))
+    c = plus(first(four(term[1:5])), on(s4, c))
+    c = tuple(x * edge for x in c)
     for _ in range(SQUARINGS):
-        r00, r01, r10, r11, c0, c1 = (
-            r00 * r00 + r01 * r10,
-            r00 * r01 + r01 * r11,
-            r10 * r00 + r11 * r10,
-            r10 * r01 + r11 * r11,
-            r00 * c0 + r01 * c1 + c0,
-            r10 * c0 + r11 * c1 + c1,
-        )
-    return r00, r10, c0, c1
+        r, c = times(r, r), plus(on(r, c), c)
+    return r[0], r[2], c[0], c[1]
 
 
 def kernel(
     members, rows, parts, slabs,
-    a_hbm, damp_hbm, f_hbm, c_hbm, n_ref, o_ref,
-    stage, at, xs, cb, fb, lb, pu, pa, gf, gu, ck, tb, tf, tp, ls, damp_ref,
+    a_hbm, damp_hbm, f_hbm, c_hbm, n_hbm, o_ref,
+    stage, at, xs, cb, fb, lb, pu, pa, gf, gu, ck, tb, tf, tp, ls, damp_ref, n_ref,
     a_sem, small_sem, ready, send, recv, recv_one,
 ):
     t, r = lax.axis_index("tm"), lax.axis_index("row")
@@ -83,7 +89,7 @@
     small = [
         pltpu.make_async_copy(from_ref, to_ref, small_sem.at[i])
         for i, (from_ref, to_ref) in enumerate(
-            ((f_hbm, fb.at[OWN]), (c_hbm, cb.at[OWN]), (damp_hbm, damp_ref))
+            ((f_hbm, fb.at[OWN]), (c_hbm, cb.at[OWN]), (damp_hbm, damp_ref), (n_hbm, n_ref))
         )
     ]
 
@@ -128,17 +134,33 @@
         some = buffer.at[pl.ds(0, count)]
         pltpu.make_async_copy(some, some, semaphore).wait()
 
+    def all_left(first, second):
+        for buffer, k in ((fb, F), (gf, GF), (gu, GU), (tb, TB)):
+            took(buffer, send.at[k], last)
+        if first or second:
+            took(cb, send.at[C], last)
+        if not first:
+            for buffer, k in ((lb, LB), (pu, PU), (pa, PA), (tf, TF)):
+                took(buffer, send.at[k], last)
+
+        @pl.when(t + 1 < slabs)
+        def _():
+            for k in (LBR, PUR, PAR):
+                took(lb, send.at[k], 1)
+            took(tp, send.at[TP], parts)
+
     def fill(slot, at_part, v):
         high = v.astype(jnp.bfloat16).astype(jnp.float32)
         both = jnp.concatenate([high, v - high], axis=0).astype(jnp.bfloat16)
         xs[16 * slot : 16 * slot + 16, rows * at_part : rows * at_part + rows] = both
 
-    def applied(*gathers):
+    def applied(*gathers, forwarded=False, then=None):
         count = len(gathers)
         total = jnp.zeros((2 * members * count, 2 * rows), jnp.float32)
         norms, d = {}, {}
         for j, (buffer, k, *beside) in enumerate(gathers):
-            forward(buffer, k)
+            if not forwarded:
+                forward(buffer, k)
             if beside:
                 n2 = jnp.zeros((members, rows), jnp.float32)
                 d[j] = jnp.zeros((members, rows), jnp.float32)
@@ -163,6 +185,8 @@
                 xs[0 : 16 * count, rows * low : rows * high], at[rows * low : rows * high, :],
                 preferred_element_type=jnp.float32,
             )
+            if group == 0 and then is not None:
+                then()
         out = []
         for j, (buffer, _, *beside) in enumerate(gathers):
             at_row = 2 * members * j
@@ -180,7 +204,9 @@
         for p in range(parts):
             w = second[p] - g * first[p]
             w2 += w * w
-        return jnp.sqrt(jnp.sum(w2, axis=1, keepdims=True) / b2 + EPSILON)
+        side = jnp.sqrt(jnp.sum(w2, axis=1, keepdims=True) / b2 + EPSILON)
+        inverse = 1.0 / side
+        return g, side, inverse, inverse / b2
 
     def sums(first, second, image, g):
         w = second - g * first
@@ -201,41 +227,43 @@
         return jnp.sum(row, axis=0, keepdims=True)
 
     def unpacked(buffer, count):
-        total = jnp.sum(buffer[...], axis=0)
-        total = jnp.broadcast_to(total, (members, LANES))
+        parts_of = [buffer[p] for p in range(parts)]
+        while len(parts_of) > 1:
+            parts_of = [a + b for a, b in zip(parts_of[::2], parts_of[1::2])]
+        total = jnp.broadcast_to(parts_of[0], (members, LANES))
         return [
             jnp.sum(jnp.where(lane == member + members * j, total, 0.0), axis=1, keepdims=True)
             for j in range(count)
         ]
 
     def start_weights(h, known, t0, t1):
-        b2, g, side = known
-        e00, e10, _, _ = exponential(h, g, side, t0 / (b2 * side), t1 / (b2 * side * side))
-        x2 = e10 / side
+        g, side, inverse, unit = known
+        e00, e10, _, _ = exponential(h, g, side, t0 * unit, (t1 * unit) * inverse)
+        x2 = e10 * inverse
         return e00 - g * x2, x2
 
     def forcing_weights(h, known, t0, t1):
-        b2, g, side = known
-        _, _, c0, c1 = exponential(h, g, side, t0 / (b2 * side), t1 / (b2 * side * side))
-        x4 = h * c1 / side
+        g, side, inverse, unit = known
+        _, _, c0, c1 = exponential(h, g, side, t0 * unit, (t1 * unit) * inverse)
+        x4 = h * c1 * inverse
         return h * c0 - g * x4, x4
+
+    barrier = pltpu.get_barrier_semaphore()
+    for i in (*range(OWN), last):
+        pl.semaphore_signal(barrier, inc=1, device_id=(t, device(i)), device_id_type=MESH)
+
+    @pl.when(t > 0)
+    def _():
+        pl.semaphore_signal(barrier, inc=1, device_id=(t - 1, r), device_id_type=MESH)
+
+    @pl.when(t + 1 < slabs)
+    def _():
+        pl.semaphore_signal(barrier, inc=1, device_id=(t + 1, r), device_id_type=MESH)
 
     for copy_in in small:
         copy_in.start()
     for j in range(CHUNKS):
         loads(j).start()
-
-    barrier = pltpu.get_barrier_semaphore()
-    for i in (*range(OWN), last):
-        pl.semaphore_signal(barrier, inc=1, device_id=(t, device(i)), device_id_type=MESH)
-
-    @pl.when(t > 0)
-    def _():
-        pl.semaphore_signal(barrier, inc=1, device_id=(t - 1, r), device_id_type=MESH)
-
-    @pl.when(t + 1 < slabs)
-    def _():
-        pl.semaphore_signal(barrier, inc=1, device_id=(t + 1, r), device_id_type=MESH)
 
     for copy_in in small:
         copy_in.wait()
@@ -256,7 +284,9 @@
 
     for j in range(CHUNKS):
         loads(j).wait()
-    for i, (dz, dy, flip) in enumerate(STEPS):
+
+    def convert(i):
+        dz, dy, flip = STEPS[i]
         source = zs[(SIDE - dz) % SIDE] + ys[(SIDE - dy) % SIDE] + cores[flip]
         block = stage[:, pl.ds(pl.multiple_of(source * rows, rows), rows)].T
         high = block.astype(jnp.bfloat16)
@@ -265,29 +295,44 @@
             jnp.bfloat16
         )
 
+    for i in range(parts - LATE):
+        convert(i)
+
+    @pl.when(t == 0)
+    def _():
+        forward(cb, C)
+
+    @pl.when(t > 0)
+    def _():
+        forward(fb, F)
+
+    for i in range(parts - LATE, parts):
+        convert(i)
+
     own_f = fb[OWN]
 
     @pl.when(t == 0)
     def _():
         own_c = cb[OWN]
-        image_c = applied((cb, C))
+        image_c = applied((cb, C), forwarded=True, then=lambda: forward(fb, F))
         gu[OWN] = image_c
         relay(gu.at[OWN], pu, PUR).start()
         spread(gu, GU)
-        image_f = applied((fb, F))
+        image_f = applied((fb, F), forwarded=True)
         gf[OWN] = image_f
         relay(gf.at[OWN], pa, PAR).start()
         spread(gf, GF)
         image, b2, g = applied((gu, GU, cb))
         t0c, t1c = sums(own_c, image_c, image, g)
-        known_c = (b2, g, below(cb, gu, b2, g))
+        known_c = below(cb, gu, b2, g)
         image, b2, g = applied((gf, GF, fb))
         t0f, t1f = sums(own_f, image_f, image, g)
         tb[OWN] = packed([t0c, t1c, t0f, t1f, h])
         pl.semaphore_wait(ready, 1)
         spread_next()
         spread_sums(tb, TB)
-        known_f = (b2, g, below(fb, gf, b2, g))
+        known_f = below(fb, gf, b2, g)
+        all_left(True, False)
         took(tb, recv_one.at[TB], last)
         t0c, t1c, t0f, t1f = unpacked(tb, 4)
         x1, x2 = start_weights(h, known_c, t0c, t1c)
@@ -301,18 +346,18 @@
 
         if early:
             pass_on(lb, LBR, LB)
-        image_f = applied((fb, F))
+        image_f = applied((fb, F), forwarded=True, then=(lambda: forward(cb, C)) if early else None)
         pl.semaphore_signal(ready, inc=1, device_id=(t - 1, r), device_id_type=MESH)
         gf[OWN] = image_f
         spread(gf, GF)
         if early:
-            image_c = applied((cb, C))
+            image_c = applied((cb, C), forwarded=True)
             pass_on(pu, PUR, PU)
             pass_on(pa, PAR, PA)
         image, b2, g = applied((gf, GF, fb))
         tf[OWN] = packed(list(sums(own_f, image_f, image, g)))
         spread_sums(tf, TF)
-        known_f = (b2, g, below(fb, gf, b2, g))
+        known_f = below(fb, gf, b2, g)
 
         def finish_forcing():
             took(tf, recv_one.at[TF], last)
@@ -329,8 +374,8 @@
         if early:
             image_l = applied((lb, LB))
             (image_u, b2c, gc), (image_p, b2l, gl) = applied((pu, PU, cb), (pa, PA, lb))
-            known_c = (b2c, gc, below(cb, pu, b2c, gc))
-            known_l = (b2l, gl, below(lb, pa, b2l, gl))
+            known_c = below(cb, pu, b2c, gc)
+            known_l = below(lb, pa, b2l, gl)
             local = finish_forcing()
         else:
             local = finish_forcing()
@@ -338,7 +383,7 @@
             pass_on(pu, PUR, PU)
             pass_on(pa, PAR, PA)
             image_l, image_p, (image_u, b2c, gc) = applied((lb, LB), (pa, PA), (pu, PU, pa))
-            known_c = (b2c, gc, below(pa, pu, b2c, gc))
+            known_c = below(pa, pu, b2c, gc)
         took(tp, recv_one.at[TP], parts)
         t0c, t1c, t0l, t1l, hs = unpacked(tp, 5)
         hs = hs * (1.0 / parts)
@@ -372,7 +417,8 @@
             spread_next()
 
         spread_sums(tb, TB)
-        known = (b2, g, below(ck, gu, b2, g))
+        known = below(ck, gu, b2, g)
+        all_left(False, early)
         took(tb, recv_one.at[TB], last)
         x1, x2 = start_weights(h, known, *unpacked(tb, 2))
         o_ref[...] = x1 * own + x2 * image + local
@@ -380,35 +426,17 @@
     pl.when(t == 1)(functools.partial(later, True))
     pl.when(t > 1)(functools.partial(later, False))
 
-    for buffer, k in ((fb, F), (gf, GF), (gu, GU), (tb, TB)):
-        took(buffer, send.at[k], last)
-
-    @pl.when(t < 2)
-    def _():
-        took(cb, send.at[C], last)
-
-    @pl.when(t + 1 < slabs)
-    def _():
-        for k in (LBR, PUR, PAR):
-            took(lb, send.at[k], 1)
-        took(tp, send.at[TP], parts)
-
-    @pl.when(t > 0)
-    def _():
-        for buffer, k in ((lb, LB), (pu, PU), (pa, PA), (tf, TF)):
-            took(buffer, send.at[k], last)
-
 
 def on_device(parts, slabs, coupling, damping, forcing, initial, counts):
     members, rows = initial.shape
     whole = coupling.shape[2]
-    far, ram = pl.BlockSpec(memory_space=pl.ANY), pl.BlockSpec(memory_space=pltpu.SMEM)
+    far = pl.BlockSpec(memory_space=pl.ANY)
     blocks = pltpu.VMEM((parts, members, rows), jnp.float32)
     scalars = pltpu.VMEM((parts, 1, LANES), jnp.float32)
     result = pl.pallas_call(
         functools.partial(kernel, members, rows, parts, slabs),
         out_shape=jax.ShapeDtypeStruct((members, rows), jnp.float32),
-        in_specs=[far, far, far, far, ram],
+        in_specs=[far] * 5,
         out_specs=pl.BlockSpec(memory_space=pltpu.VMEM),
         scratch_shapes=[
             pltpu.VMEM((rows, whole), jnp.float32),
@@ -418,8 +446,9 @@
             *[scalars] * 3,
             pltpu.VMEM((members, rows), jnp.float32),
             pltpu.VMEM((1, rows), jnp.float32),
+            pltpu.SMEM((1,), jnp.int32),
             pltpu.SemaphoreType.DMA((CHUNKS,)),
-            pltpu.SemaphoreType.DMA((3,)),
+            pltpu.SemaphoreType.DMA((4,)),
             pltpu.SemaphoreType.REGULAR,
             pltpu.SemaphoreType.DMA((13,)),
             pltpu.SemaphoreType.DMA((7, 2 * len(GROUPS))),

time: 64.8 us -> 64.6 us (level)
  no operation moved by 1% of the time
where the time goes in v4:
time: 64.6 us; the launch traced here: 64.5 us
  Pallas kernels  62.5 us (97%)
  local copies, waits for them, and re-layouts  1.3 us (2%)
  between operations  0.66 us (1%)
    pallas_call x1, Pallas kernels, on_device(): pl.pallas_call(functools.partial(kernel, members, rows, parts, slabs), ou...  62.5 us
    unnamed x1, local copies, waits for them, and re-layouts  1.3 us

profile of v4, /device:TPU:6, one launch (start us, length us, event | category | flops | bytes accessed | tf_op | source)
XLA Modules:
  0.0 64.5 jit_solution(2044294738069119835)
XLA Ops:
  0.7 62.5 %shard_map.55 = f32[8,256]{1,0:T(8,128)} custom-call(f32[1,256,8192]{2,1,0:T(8,128)} %a_hbm.1, f32[1,256]{1,0:T(1,128)} %damp_hbm.1, f32[8,256]{1,0:T(8,128)} %bitcast.3, f32[8,256]{1,0:T(8,128)} %c_hbm.1, s32[1]{0:T(128)S(6)} %copy.7.n_hbm), custom_call_target="tpu_custom_call" | custom-call | tf_op jit(solution)/shard_map/pallas_call | solution.py:436
  63.2 1.3 %copy.8 = f32[1,8,256]{2,1,0:T(8,128)} copy(f32[1,8,256]{2,1,0:T(8,128)} %bitcast.2) | data formatting | bytes 16384
